TPU v7x, 32 devices: a whole 2x2x4 slice. The times are simulated.
32 devices in a mesh: groups: 2 (over x), tm: 16 (over z, y, core).
Axes of the slice: x: 2, y: 2, z: 4, core: 2. Of those that a mesh axis runs over, the one named last changes fastest.
Arguments:
- coupling: bfloat16 [1024, 1024], replicated, may hold values from -0.0546875 to 0.0546875
- decay: float32 [32, 1024], P(('groups', 'tm')), parts along dimension 0, may hold values from 0.3 to 1
- block_mask: int32 [32, 8, 8], P(('groups', 'tm')), parts along dimension 0, may hold values 0 or 1
- gain: bfloat16 [1024, 256], replicated, may hold values from -0.375 to 0.375
- readings: bfloat16 [32, 256, 2048], P(('groups', 'tm')), parts along dimension 0, may hold values from -6 to 6
- influence: float32 [1024, 4], replicated, may hold values from -6 to 6
- lanes: int32 [32, 2048], P(('groups', 'tm')), parts along dimension 0, may hold values from 0 to 3
- axle_load: float32 [32, 2048], P(('groups', 'tm')), parts along dimension 0, may hold values from -6 to 6
Outputs:
- states: float32 [32, 1024, 2048], P(('groups', 'tm')), parts along dimension 0
There are 2 independent parts, one for each index of `groups`. A program takes and returns all parts, laid end to end along the dimension named above; an argument that names none is the same for every part. Nothing has to cross between parts.
Inputs may be any that keep to these rules, and one draw needn't show every extreme that they name: `block_mask`: 1 where the time block couples a block of states to another.
All inputs are finite; a program needn't handle non-finite values.
Results may differ from a plain program's by a relative error of at most 0.006.
Values may be sent and summed in bfloat16 or wider, within the bound.
No kernel may reach another device: no remote copies, remote signals or barrier semaphores. Data moves between devices by JAX's collectives and lax.ppermute only.
A program may use at most 64 MiB of HBM per device.

v0:
```python
import jax
import jax.numpy as jnp
from jax import lax
from jax.sharding import PartitionSpec as P


def shifted(block, axis, distance):
    devices = range(lax.axis_size(axis))
    route = [(i - distance, i) for i in devices if i - distance in devices]
    return lax.ppermute(block, axis, route)


def build(coupling, rate_row, mask_row):
    blocks = mask_row.shape[0]
    width = coupling.shape[0]
    size = width // blocks
    masked = (
        coupling.astype(jnp.float32).reshape(blocks, size, blocks, size)
        * mask_row.astype(jnp.float32)[:, None, :, None]
    )
    return (masked.reshape(width, width) + jnp.diag(rate_row.astype(jnp.float32))).astype(
        jnp.bfloat16
    )


def product(left, right):
    return jnp.dot(left, right, preferred_element_type=jnp.float32)


def make_drive(gain, influence, sensor_rows, lane_row, load_row):
    lane_count = influence.shape[1]
    picks = (lane_row[None, :] == jnp.arange(lane_count, dtype=jnp.float32)[:, None]).astype(
        jnp.float32
    ) * load_row[None, :]
    return product(gain, sensor_rows) + jnp.dot(influence, picks, precision=lax.Precision.HIGHEST)


def per_device(coupling, decay, block_mask, gain, readings, influence, lanes, axle_load):
    rate = decay[0].astype(jnp.bfloat16)
    mask_half = block_mask[0].astype(jnp.bfloat16)
    trans = build(coupling, rate, mask_half)
    lane_values = lanes[0].astype(jnp.float32)
    drive = make_drive(gain, influence, readings[0], lane_values, axle_load[0])
    drive_half = drive.astype(jnp.bfloat16)
    prev_trans, prev_vec = shifted((trans, drive_half), "tm", 1)
    pair = product(trans, prev_trans).astype(jnp.bfloat16)
    sum_one = drive + product(trans, prev_vec)
    one_half = sum_one.astype(jnp.bfloat16)
    far_pair, far_vec = shifted((pair, one_half), "tm", 2)
    sum_two = sum_one + product(pair, far_vec)
    last_vec = shifted(sum_two.astype(jnp.bfloat16), "tm", 4)
    quad = product(pair, far_pair).astype(jnp.bfloat16)
    states = sum_two + product(quad, last_vec)
    return states[None]


def solution(mesh):
    placed = (
        P(),
        P(("groups", "tm"), None),
        P(("groups", "tm"), None, None),
        P(),
        P(("groups", "tm"), None, None),
        P(),
        P(("groups", "tm"), None),
        P(("groups", "tm"), None),
    )
    return jax.shard_map(
        per_device,
        mesh=mesh,
        in_specs=placed,
        out_specs=P(("groups", "tm"), None, None),
        check_vma=False,
    )
```

profile of v0, /device:TPU:16, one launch (start us, length us, event | category | flops | bytes accessed | tf_op | source)
XLA Modules:
  0.0 348.4 jit_solution(17066931214231272138)
XLA Ops:
  0.0 0.0 copy-start
  0.0 0.8 convert_element_type.62
  0.8 0.4 copy-done
  1.2 0.0 copy-start.3
  1.2 0.0 copy-start.4
  1.2 2.3 fusion.5
  3.6 0.0 copy-done.3
  3.6 0.0 copy-done.4
  3.6 0.0 copy-start.5
  3.6 0.0 copy-start.6
  3.6 7.0 %fusion.12 = (bf16[1024,2048]{1,0:T(8,128)(2,1)S(1)}, f32[1024,2048]{1,0:T(8,128)S(1)}) fusion(f32[1024,2048]{1,0:T(8,128)S(1)} %fusion.5, f32[1024,4]{0,1:T(4,128)S(1)} %copy-done.3, f32[2048]{0:T(1024)S(1)} %bitcast.35, f32[2048]{0:T(1024)S(1)} %bitcast.33), kind=kOutput, calls=%fused_computation.21 | convolution fusion | flops 104873984 | bytes 21004288 | tf_op jit(solution)/shard_map/dot_general | solution.py:35
  10.6 0.0 copy-start.2
  10.7 2.2 collective-permute-start
  12.9 0.0 copy-done.5
  12.9 0.0 copy-done.6
  12.9 0.3 mul.24
  13.3 0.0 copy-done.2
  13.3 1.4 fusion.1
  14.7 46.9 %collective-permute-done = bf16[1024,2048]{1,0:T(8,128)(2,1)S(1)} collective-permute-done((bf16[1024,2048]{1,0:T(8,128)(2,1)S(1)}, bf16[1024,2048]{1,0:T(8,128)(2,1)S(1)}, u32[]{:S(2)}, u32[]{:S(2)}) %collective-permute-start) | collective-permute-done | bytes 4194336 | tf_op jit(solution)/shard_map/ppermute | solution.py:10
  61.5 6.7 %fusion.13 = (bf16[1024,2048]{1,0:T(8,128)(2,1)S(1)}, f32[1024,2048]{1,0:T(8,128)}) fusion(f32[1024,2048]{1,0:T(8,128)S(1)} %get-tuple-element.6, bf16[1024,1024]{1,0:T(8,128)(2,1)S(1)} %fusion.1, bf16[1024,2048]{1,0:T(8,128)(2,1)S(1)} %collective-permute-done), kind=kOutput, calls=%fused_computation.22 | convolution fusion | flops 4299161600 | bytes 27262976 | tf_op jit(solution)/shard_map/dot_general | solution.py:27
  68.2 0.0 copy-start.9
  68.2 2.9 collective-permute-start.2
  71.1 1.9 collective-permute-start.1
  73.1 111.4 %collective-permute-done.1 = bf16[1024,1024]{1,0:T(8,128)(2,1)S(1)} collective-permute-done((bf16[1024,1024]{1,0:T(8,128)(2,1)S(1)}, bf16[1024,1024]{1,0:T(8,128)(2,1)S(1)}, u32[]{:S(2)}, u32[]{:S(2)}) %collective-permute-start.1) | collective-permute-done | bytes 2097184 | tf_op jit(solution)/shard_map/ppermute | solution.py:10
  184.5 2.4 convolution_convert_fusion
  186.8 0.0 collective-permute-done.2
  186.8 0.0 copy-done.9
  186.8 6.7 %fusion.14 = (bf16[1024,2048]{1,0:T(8,128)(2,1)S(1)}, f32[1024,2048]{1,0:T(8,128)}) fusion(f32[1024,2048]{1,0:T(8,128)S(1)} %copy-done.9, bf16[1024,1024]{1,0:T(8,128)(2,1)S(1)} %convolution_convert_fusion, bf16[1024,2048]{1,0:T(8,128)(2,1)S(1)} %collective-permute-done.2), kind=kOutput, calls=%fused_computation.23 | convolution fusion | flops 4299161600 | bytes 27262976 | tf_op jit(solution)/shard_map/dot_general | solution.py:27
  193.5 3.5 collective-permute-start.4
  197.0 1.9 collective-permute-start.3
  199.0 133.1 %collective-permute-done.3 = bf16[1024,1024]{1,0:T(8,128)(2,1)S(1)} collective-permute-done((bf16[1024,1024]{1,0:T(8,128)(2,1)S(1)}, bf16[1024,1024]{1,0:T(8,128)(2,1)S(1)}, u32[]{:S(2)}, u32[]{:S(2)}) %collective-permute-start.3) | collective-permute-done | bytes 2097184 | tf_op jit(solution)/shard_map/ppermute | solution.py:10
  332.1 0.0 copy-start.8
  332.1 0.0 collective-permute-done.4
  332.1 1.3 copy-done.8
  333.4 0.0 copy-start.7
  333.4 2.0 copy-done.7
  335.4 0.0 copy-start.1
  335.4 13.0 %add_bitcast_fusion = f32[1,1024,2048]{2,1,0:T(8,128)} fusion(f32[1024,2048]{1,0:T(8,128)} %get-tuple-element.10, bf16[1024,2048]{1,0:T(8,128)(2,1)} %copy-done.7, bf16[1024,1024]{1,0:T(8,128)(2,1)S(1)} %convolution_convert_fusion, bf16[1024,1024]{1,0:T(8,128)(2,1)} %copy-done.8), kind=kOutput, calls=%fused_computation.1 | convolution fusion | flops 6445596672 | bytes 25165824 | tf_op jit(solution)/shard_map/dot_general | solution.py:27
  348.4 0.0 copy-done.1
  (2 shorter events, 0.0 us)
Async XLA Ops:
  0.0 1.2 copy-start
  1.2 2.3 copy-start.3
  1.2 2.3 copy-start.4
  3.6 9.3 %copy-start.5 = (s32[1,8,8]{2,1,0:T(8,128)S(1)}, s32[1,8,8]{2,1,0:T(8,128)}, u32[]{:S(2)}) copy-start(s32[1,8,8]{2,1,0:T(8,128)} %param.10) | copy-start | bytes 772
  3.6 9.3 %copy-start.6 = (f32[1,1024]{1,0:T(1,128)S(1)}, f32[1,1024]{1,0:T(1,128)}, u32[]{:S(2)}) copy-start(f32[1,1024]{1,0:T(1,128)} %param.9) | copy-start | bytes 12292
  10.6 2.6 copy-start.2
  10.7 50.9 %collective-permute-start = (bf16[1024,2048]{1,0:T(8,128)(2,1)S(1)}, bf16[1024,2048]{1,0:T(8,128)(2,1)S(1)}, u32[]{:S(2)}, u32[]{:S(2)}) collective-permute-start(bf16[1024,2048]{1,0:T(8,128)(2,1)S(1)} %get-tuple-element.5), channel_id=1, source_target_pairs={{0,1},{1,2},{2,3},{3,4},{4,5},{5,6},{6,7},{7,8},{8,9},{9,10},{10,1... | collective-permute-start | bytes 12582920 | tf_op jit(solution)/shard_map/ppermute | solution.py:10
  68.2 118.6 %copy-start.9 = (f32[1024,2048]{1,0:T(8,128)S(1)}, f32[1024,2048]{1,0:T(8,128)}, u32[]{:S(2)}) copy-start(f32[1024,2048]{1,0:T(8,128)} %get-tuple-element.8) | copy-start | bytes 25165828
  68.2 118.6 %collective-permute-start.2 = (bf16[1024,2048]{1,0:T(8,128)(2,1)S(1)}, bf16[1024,2048]{1,0:T(8,128)(2,1)S(1)}, u32[]{:S(2)}, u32[]{:S(2)}) collective-permute-start(bf16[1024,2048]{1,0:T(8,128)(2,1)S(1)} %get-tuple-element.7), channel_id=1, source_target_pairs={{0,2},{1,3},{2,4},{3,5},{4,6},{5,7},{6,8},{7,9},{8,10},{9,11},{10,... | collective-permute-start | bytes 12582920 | tf_op jit(solution)/shard_map/ppermute | solution.py:10
  71.1 113.3 %collective-permute-start.1 = (bf16[1024,1024]{1,0:T(8,128)(2,1)S(1)}, bf16[1024,1024]{1,0:T(8,128)(2,1)S(1)}, u32[]{:S(2)}, u32[]{:S(2)}) collective-permute-start(bf16[1024,1024]{1,0:T(8,128)(2,1)S(1)} %fusion.1), channel_id=1, source_target_pairs={{0,1},{1,2},{2,3},{3,4},{4,5},{5,6},{6,7},{7,8},{8,9},{9,10},{10,1... | collective-permute-start | bytes 6291464 | tf_op jit(solution)/shard_map/ppermute | solution.py:10
  193.5 138.5 %collective-permute-start.4 = (bf16[1024,2048]{1,0:T(8,128)(2,1)S(1)}, bf16[1024,2048]{1,0:T(8,128)(2,1)S(1)}, u32[]{:S(2)}, u32[]{:S(2)}) collective-permute-start(bf16[1024,2048]{1,0:T(8,128)(2,1)S(1)} %get-tuple-element.9), channel_id=1, source_target_pairs={{0,4},{1,5},{2,6},{3,7},{4,8},{5,9},{6,10},{7,11},{8,12},{9,13},{1... | collective-permute-start | bytes 12582920 | tf_op jit(solution)/shard_map/ppermute | solution.py:10
  197.0 135.0 %collective-permute-start.3 = (bf16[1024,1024]{1,0:T(8,128)(2,1)S(1)}, bf16[1024,1024]{1,0:T(8,128)(2,1)S(1)}, u32[]{:S(2)}, u32[]{:S(2)}) collective-permute-start(bf16[1024,1024]{1,0:T(8,128)(2,1)S(1)} %convolution_convert_fusion), channel_id=1, source_target_pairs={{0,2},{1,3},{2,4},{3,5},{4,6},{5,7},{6,8},{7,9},{8,10},{9,11},{10,... | collective-permute-start | bytes 6291464 | tf_op jit(solution)/shard_map/ppermute | solution.py:10
  332.1 1.4 copy-start.8
  333.4 2.0 copy-start.7
  335.4 13.0 %copy-start.1 = (bf16[1,256,2048]{2,1,0:T(8,128)(2,1)S(1)}, bf16[1,256,2048]{2,1,0:T(8,128)(2,1)}, u32[]{:S(2)}) copy-start(bf16[1,256,2048]{2,1,0:T(8,128)(2,1)} %param.12) | copy-start | bytes 3145732
where the time goes:
time: 349 us; the launch traced here: 348 us
  waiting for transfers between devices  291 us (83%)
  matrix products  38.1 us (11%)
  starting transfers between devices  12.5 us (4%)
  local copies, waits for them, and re-layouts  4.13 us (1%)
    ppermute x5, waiting for transfers between devices, shifted(): return lax.ppermute(block, axis, route)  291 us
    dot_general x5, matrix products, product(): return jnp.dot(left, right, preferred_element_type=jnp.float32)  31.1 us
    ppermute x5, starting transfers between devices, shifted(): return lax.ppermute(block, axis, route)  12.5 us
    dot_general x1, matrix products, make_drive(): jnp.dot(influence, picks, precision=lax.Precision.HIGHEST)  7.02 us
  transfers between devices with their start and end apart: 5, of which 3 were waited for; matrix products, arithmetic and copies ran while one was open for 1% of the time, Pallas kernels for 0%

commit v1 on v0

v1 whole, which is shorter than its diff:
```python
import functools

import jax
import jax.numpy as jnp
from jax import lax
from jax.experimental import pallas as pl
from jax.experimental.pallas import tpu as pltpu
from jax.sharding import PartitionSpec as P

MIB = 1 << 20
VMEM = pl.BlockSpec(memory_space=pltpu.VMEM)
ANY = pl.BlockSpec(memory_space=pl.ANY)
F32 = jnp.float32
BF16 = jnp.bfloat16
LAGS = 8
ROWS = 16


def position():
    return lax.rem(lax.axis_index("tm"), 4)


def send(block, pairs, levels):
    count = lax.axis_size("tm")
    route = []
    for level in range(count // 4):
        for a, b, step in pairs:
            if level + step < count // 4:
                route.append((level * 4 + a, (level + step) * 4 + b))
    return lax.ppermute(block, "tm", route)


CORE = [(0, 1, 0), (1, 0, 0), (2, 3, 0), (3, 2, 0)]
ROW = [(0, 2, 0), (2, 0, 0), (1, 3, 0), (3, 1, 0)]
ROW0 = [(0, 2, 0), (2, 0, 0)]
ROW1 = [(1, 3, 0), (3, 1, 0)]


def record_of(j, lag, recs):
    d = j - lag
    pos = lax.rem(d + 8, 4)
    here = recs[0][pos ^ j]
    base = j | 1
    row = jnp.where(d >= 0, here, recs[1][pos ^ base])
    if len(recs) > 2:
        row = jnp.where(d >= -4, row, recs[2][pos ^ base])
    return row.astype(F32)


def build(c_ref, rec, t_ref):
    width = c_ref.shape[0]
    size = width // 8
    eye = (
        lax.broadcasted_iota(jnp.int32, (size, size), 0)
        == lax.broadcasted_iota(jnp.int32, (size, size), 1)
    ).astype(F32)
    for p in range(8):
        rows = slice(p * size, (p + 1) * size)
        masked = c_ref[rows, :].astype(F32) * rec[p : p + 1, :]
        t_ref[rows, :] = masked.astype(BF16)
        rate = rec[8:9, p * size : (p + 1) * size]
        t_ref[rows, rows] = (masked[:, rows] + eye * rate).astype(BF16)


def times(left, right):
    return jnp.dot(left, right, preferred_element_type=F32)


def keep(m_ref, w, value, lag, sens):
    m_ref[:, lag * sens : (lag + 1) * sens] = value[:, :sens].astype(BF16)
    lanes = lax.broadcasted_iota(jnp.int32, w.shape, 1)
    mine = ((lanes & 31) >> 2) == lag
    return jnp.where(mine, value[:, sens:], w)


def extend(p_ref, t_ref, out_ref):
    width = p_ref.shape[0]
    for n in range(0, width, 256):
        out_ref[:, n : n + 256] = times(p_ref[...], t_ref[:, n : n + 256]).astype(BF16)


def first_kernel(c, gi, inf, s0, s1, m, w, p2, t1, t2):
    sens = gi.shape[1] - 128
    j = position()
    m[:, :sens] = gi[:, :sens]
    build(c, record_of(j, 0, (s0, s1)), t1)
    acc = keep(m, inf[...], times(t1[...], gi[...]), 1, sens)
    build(c, record_of(j, 1, (s0, s1)), t2)
    extend(t1, t2, p2)
    w[...] = keep(m, acc, times(p2[...], gi[...]), 2, sens)


def next_kernel(lag, c, gi, s0, s1, p, m_in, w_in, m, w, q, t):
    del m_in
    sens = gi.shape[1] - 128
    build(c, record_of(position(), lag, (s0, s1)), t)
    extend(p, t, q)
    w[...] = keep(m, w_in[...], times(q[...], gi[...]), lag + 1, sens)


def far_kernel(c, gi, s0, s1, s2, f5, f6, f7, fw, t):
    sens = gi.shape[1] - 128
    j = position()
    recs = (s0, s1, s2)
    f7[...] = gi[:, :sens]
    f6[...] = gi[:, :sens]
    f5[...] = gi[:, :sens]
    fw[...] = gi[:, sens:]
    lanes = lax.broadcasted_iota(jnp.int32, fw.shape, 1)
    group = (lanes & 31) >> 2
    for lag in (6, 5, 4):
        build(c, record_of(j, lag, recs), t)
        f7[...] = times(t[...], f7[...]).astype(BF16)
        if lag < 6:
            f6[...] = times(t[...], f6[...]).astype(BF16)
        if lag < 5:
            f5[...] = times(t[...], f5[...]).astype(BF16)
        fw[...] = jnp.where(group > lag, times(t[...], fw[...]).astype(BF16), fw[...])


def near_kernel(p, f5, f6, f7, fw, m_in, w_in, m, w):
    del m_in
    sens = f5.shape[1]
    for lag, f in ((5, f5), (6, f6), (7, f7)):
        m[:, lag * sens : (lag + 1) * sens] = times(p[...], f[...]).astype(BF16)
    lanes = lax.broadcasted_iota(jnp.int32, w_in.shape, 1)
    full = jnp.where(((lanes & 31) >> 2) >= 5, times(p[...], fw[...]), w_in[...])
    high = full.astype(BF16)
    low = (full - high.astype(F32)).astype(BF16)
    w[...] = jnp.where(lanes < 64, high, jnp.where(lanes < 96, low, jnp.zeros_like(low)))


def picks_kernel(s0, s1, s2, out, tmp):
    j = position()
    half = s0.shape[2]
    tmp[96:, :] = jnp.zeros_like(tmp[96:, :])
    for lag in range(LAGS):
        rec = record_of(j, lag, (s0, s1, s2))
        for h in range(2):
            cols = slice(h * half, (h + 1) * half)
            lane = lax.broadcasted_iota(jnp.int32, (4, half), 0).astype(F32)
            mine = lane == rec[9 + h : 10 + h, :]
            high = jnp.where(mine, rec[11 + h : 12 + h, :], 0.0)
            low = jnp.where(mine, rec[13 + h : 14 + h, :], 0.0)
            tmp[4 * lag : 4 * lag + 4, cols] = high
            tmp[32 + 4 * lag : 36 + 4 * lag, cols] = low
            tmp[64 + 4 * lag : 68 + 4 * lag, cols] = high
    out[...] = tmp[...].astype(BF16)


EARLY = {
    0: [(0, "O"), (1, "CYR2"), (2, "YR1"), (3, "CR2"), (4, "R1")],
    1: [(0, "O"), (1, "CO"), (2, "YR2"), (3, "CYR1"), (4, "R2"), (5, "CR1")],
    2: [(0, "O"), (2, "YO1"), (3, "CR2"), (4, "R1"), (5, "CYR2"), (6, "YR1")],
    3: [(0, "O"), (1, "CO"), (3, "CYO1"), (4, "R2"), (5, "CR1"), (6, "YR2"), (7, "CYR1")],
}
LATE = {
    0: [(5, "Y6"), (6, "CZ3"), (7, "Z2")],
    1: [(6, "CY6"), (7, "Z3")],
    2: [(1, "CYO2"), (7, "Z2")],
    3: [(2, "YO2")],
}


def names_of(table):
    return sorted({name for entries in table.values() for _, name in entries})


def runs_of(entries):
    runs = []
    for lag, _ in entries:
        if runs and runs[-1][1] == lag:
            runs[-1][1] = lag + 1
        else:
            runs.append([lag, lag + 1])
    return runs


def sum_kernel(table, has_loads, cols, steps, *refs):
    names = names_of(table)
    blocks = dict(zip(names, refs[: len(names)]))
    rest = list(refs[len(names) :])
    m = rest.pop(0)
    if has_loads:
        w, picks = rest.pop(0), rest.pop(0)
    else:
        start = rest.pop(0)
    out, held, sems = rest
    sens = held.shape[1] // LAGS
    j = position()
    i = pl.program_id(0)
    now = lax.rem(i, 2)

    def copies(step, slot, entries):
        where = pl.ds(pl.multiple_of(step * cols, cols), cols)
        return [
            pltpu.make_async_copy(
                blocks[name].at[:sens, where],
                held.at[slot, pl.ds(lag * sens, sens), :],
                sems.at[slot, lag],
            )
            for lag, name in entries
        ]

    for pos, entries in table.items():

        @pl.when(j == pos)
        def _(entries=entries):
            @pl.when(i == 0)
            def _():
                for copy in copies(0, 0, entries):
                    copy.start()

            @pl.when(i + 1 < steps)
            def _():
                for copy in copies(i + 1, 1 - now, entries):
                    copy.start()

            for copy in copies(i, now, entries):
                copy.wait()
            total = times(w[...], picks[...]) if has_loads else start[...]
            for lo, hi in runs_of(entries):
                total += times(
                    m[:, lo * sens : hi * sens], held[now, lo * sens : hi * sens, :]
                )
            out[...] = total


def call(kernel, outs, ins, scratch=(), aliases=None, flops=0, limit=24):
    moved = sum(a.size * a.dtype.itemsize for a in ins)
    return pl.pallas_call(
        kernel,
        out_shape=outs,
        in_specs=[VMEM] * len(ins),
        out_specs=[VMEM] * len(outs),
        scratch_shapes=list(scratch),
        input_output_aliases=aliases or {},
        cost_estimate=pl.CostEstimate(flops=flops, bytes_accessed=moved, transcendentals=0),
        compiler_params=pltpu.CompilerParams(vmem_limit_bytes=limit * MIB),
    )(*ins)


def call_sum(table, blocks, m, extra, width, scen):
    names = names_of(table)
    sens = m.shape[1] // LAGS
    cols = 512
    steps = scen // cols
    has_loads = len(extra) == 2
    full = lambda a: pl.BlockSpec(a.shape, lambda i: (0, 0), pipeline_mode=pl.Buffered(1))
    across = lambda a: pl.BlockSpec((a.shape[0], cols), lambda i: (0, i))
    specs = [ANY] * len(names) + [full(m)]
    specs += [full(extra[0]), across(extra[1])] if has_loads else [across(extra[0])]
    return pl.pallas_call(
        functools.partial(sum_kernel, table, has_loads, cols, steps),
        grid=(steps,),
        out_shape=jax.ShapeDtypeStruct((width, scen), F32),
        in_specs=specs,
        out_specs=pl.BlockSpec((width, cols), lambda i: (0, i)),
        scratch_shapes=[
            pltpu.VMEM((2, LAGS * sens, cols), BF16),
            pltpu.SemaphoreType.DMA((2, LAGS)),
        ],
        cost_estimate=pl.CostEstimate(
            flops=2 * width * scen * sens * max(len(e) for e in table.values()),
            bytes_accessed=16 * MIB,
            transcendentals=0,
        ),
        compiler_params=pltpu.CompilerParams(vmem_limit_bytes=30 * MIB),
    )(*[blocks[n] for n in names], m, *extra)


def per_device(coupling, decay, block_mask, gain, readings, influence, lanes, axle_load):
    width, sens = gain.shape
    scen = readings.shape[2]
    lane_count = influence.shape[1]
    core = lax.rem(lax.axis_index("tm"), 2)
    own = readings[0]
    shape = jax.ShapeDtypeStruct

    high = axle_load.astype(BF16)
    low = (axle_load - high.astype(F32)).astype(BF16)
    half = scen // 2
    record = jnp.concatenate(
        [
            jnp.repeat(block_mask[0].astype(BF16), width // 8, axis=1),
            decay.astype(BF16),
            lanes.astype(BF16).reshape(2, half),
            high.reshape(2, half),
            low.reshape(2, half),
            jnp.zeros((1, half), BF16),
        ],
        axis=0,
    )[None]
    spread = jnp.tile(influence, (1, 128 // lane_count))
    gi = jnp.concatenate([gain, spread.astype(BF16)], axis=1)

    r = {"O": own}
    r["R1"] = send(own, [(0, 0, 1), (2, 2, 1)], None)
    r["CO"] = send(own, CORE, None)
    pair = jnp.concatenate([record, send(record, CORE, None)], axis=0)
    s0 = jnp.concatenate([pair, send(pair, ROW, None)], axis=0)
    s1 = send(s0, [(1, 1, 1), (3, 3, 1)], None)
    s1 = jnp.where(core == 1, s1, send(s1, CORE, None))
    r["YO1"] = send(own, ROW0, None)

    small = shape((width, 128), F32)
    p_shape = shape((width, width), BF16)
    m_shape = shape((width, LAGS * sens), BF16)
    unit = 2 * width * width * 256
    t_scratch = pltpu.VMEM((width, width), BF16)

    load = jnp.concatenate([own, s1.reshape(-1, scen)], axis=0)
    r2 = send(load, [(1, 1, 1), (3, 3, 1)], None)
    m, w, p = call(
        first_kernel, [m_shape, small, p_shape], [coupling, gi, spread, s0, s1],
        [t_scratch, t_scratch], flops=8 * unit,
    )
    r["CYO1"] = send(r["YO1"], CORE, None)
    r["CR1"] = send(r["R1"], CORE, None)
    r["YR1"] = send(r["R1"], ROW0, None)
    r["CYR1"] = send(r["YR1"], CORE, None)
    r["Z3"] = send(r["YR1"], [(0, 1, 1)], None)
    r["CZ3"] = send(r["Z3"], CORE, None)
    r["R2"] = r2[:sens]
    s2 = r2[sens:].reshape(s1.shape)
    s2 = jnp.where(core == 1, s2, send(s2, CORE, None))
    r["CR2"] = send(r["R2"], CORE, None)
    r["YR2"] = send(r["R2"], ROW1, None)
    r["CYR2"] = send(r["YR2"], CORE, None)
    r["Z2"] = send(r["R2"], [(1, 0, 1), (3, 2, 1)], None)
    r["Y6"] = send(r["Z2"], [(2, 0, 0)], None)
    r["CY6"] = send(r["Y6"], CORE, None)
    r["YO2"] = send(own, [(1, 3, 0)], None)
    r["CYO2"] = send(r["YO2"], CORE, None)

    for lag in (2, 3):
        m, w, p = call(
            functools.partial(next_kernel, lag), [m_shape, small, p_shape],
            [coupling, gi, s0, s1, p, m, w], [t_scratch], {5: 0, 6: 1}, flops=6 * unit,
        )
    f_shape = shape((width, sens), BF16)
    f5, f6, f7, fw = call(
        far_kernel, [f_shape, f_shape, f_shape, shape((width, 128), BF16)],
        [coupling, gi, s0, s1, s2], [t_scratch], flops=9 * unit,
    )
    m, w = call(
        near_kernel, [m_shape, shape((width, 128), BF16)],
        [p, f5, f6, f7, fw, m, w], (), {5: 0}, flops=4 * unit,
    )
    (picks,) = call(
        picks_kernel, [shape((128, scen), BF16)], [s0, s1, s2],
        [pltpu.VMEM((128, scen), F32)], flops=MIB,
    )
    early = call_sum(EARLY, r, m, (w, picks), width, scen)
    states = call_sum(LATE, r, m, (early,), width, scen)
    return states[None]


def solution(mesh):
    placed = (
        P(),
        P(("groups", "tm"), None),
        P(("groups", "tm"), None, None),
        P(),
        P(("groups", "tm"), None, None),
        P(),
        P(("groups", "tm"), None),
        P(("groups", "tm"), None),
    )
    return jax.shard_map(
        per_device,
        mesh=mesh,
        in_specs=placed,
        out_specs=P(("groups", "tm"), None, None),
        check_vma=False,
    )
```

time: 349 us -> 116 us (0.33)
  the two profiles are of different devices: /device:TPU:16 before, /device:TPU:1 now
where the time goes in v1:
time: 116 us; the launch traced here: 114 us
  starting transfers between devices  41 us (35%)
  Pallas kernels  36.8 us (32%)
  waiting for transfers between devices  24.1 us (21%)
  local copies, waits for them, and re-layouts  5.96 us (5%)
  other arithmetic  5.59 us (5%)
    ppermute x23, starting transfers between devices, send(): return lax.ppermute(block, 'tm', route)  41 us
    ppermute x23, waiting for transfers between devices, send(): return lax.ppermute(block, 'tm', route)  24.1 us
    pallas_call x6, Pallas kernels, call(): pl.pallas_call(kernel, out_shape=outs, in_specs=[VMEM] * len(ins), out_sp...  19.8 us
    pallas_call x2, Pallas kernels, call_sum(): pl.pallas_call(functools.partial(sum_kernel, table, has_loads, cols, step...  16.9 us
    unnamed x10, local copies, waits for them, and re-layouts  4.05 us
  transfers between devices with their start and end apart: 23, of which 7 were waited for; matrix products, arithmetic and copies ran while one was open for 3% of the time, Pallas kernels for 27%

profile of v1, /device:TPU:1, one launch (start us, length us, event | category | flops | bytes accessed | tf_op | source)
XLA Modules:
  0.0 114.0 jit_solution(15305736827872680384)
XLA Ops:
  0.0 0.8 convert_reduce_fusion
  0.8 0.7 convert_bitcast_fusion
  1.5 0.1 copy.16
  1.6 0.1 broadcast_bitcast_fusion
  1.7 0.7 convert_reduce_fusion.2
  2.4 0.7 convert_element_type.26
  3.2 0.1 collective-permute-start
  3.3 1.1 %collective-permute-done = bf16[1,16,1024]{2,1,0:T(8,128)(2,1)S(1)} collective-permute-done((bf16[1,16,1024]{2,1,0:T(8,128)(2,1)S(1)}, bf16[1,16,1024]{2,1,0:T(8,128)(2,1)S(1)}, u32[]{:S(2)}, u32[]{:S(2)}) %collective-permute-start) | collective-permute-done | bytes 32800 | tf_op jit(solution)/shard_map/ppermute | solution.py:30
  4.5 2.4 %collective-permute-start.1 = (bf16[2,16,1024]{2,1,0:T(8,128)(2,1)S(1)}, bf16[2,16,1024]{2,1,0:T(8,128)(2,1)S(1)}, u32[]{:S(2)}, u32[]{:S(2)}) collective-permute-start(bf16[2,16,1024]{2,1,0:T(8,128)(2,1)S(1)} %pad_maximum_fusion.3), channel_id=1, source_target_pairs={{0,2},{2,0},{1,3},{3,1},{4,6},{6,4},{5,7},{7,5},{8,10},{10,8},{9,1... | collective-permute-start | bytes 196616 | tf_op jit(solution)/shard_map/ppermute | solution.py:30
  6.9 2.1 %collective-permute-done.1 = bf16[2,16,1024]{2,1,0:T(8,128)(2,1)S(1)} collective-permute-done((bf16[2,16,1024]{2,1,0:T(8,128)(2,1)S(1)}, bf16[2,16,1024]{2,1,0:T(8,128)(2,1)S(1)}, u32[]{:S(2)}, u32[]{:S(2)}) %collective-permute-start.1) | collective-permute-done | bytes 65568 | tf_op jit(solution)/shard_map/ppermute | solution.py:30
  9.0 2.9 %collective-permute-start.2 = (bf16[4,16,1024]{2,1,0:T(8,128)(2,1)S(1)}, bf16[4,16,1024]{2,1,0:T(8,128)(2,1)S(1)}, u32[]{:S(2)}, u32[]{:S(2)}) collective-permute-start(bf16[4,16,1024]{2,1,0:T(8,128)(2,1)S(1)} %pad_maximum_fusion.2.s0), channel_id=1, source_target_pairs={{1,5},{3,7},{5,9},{7,11},{9,13},{11,15},{17,21},{19,23},{21,25},{2... | collective-permute-start | bytes 393224 | tf_op jit(solution)/shard_map/ppermute | solution.py:30
  12.0 1.9 %collective-permute-done.2 = bf16[4,16,1024]{2,1,0:T(8,128)(2,1)S(1)} collective-permute-done((bf16[4,16,1024]{2,1,0:T(8,128)(2,1)S(1)}, bf16[4,16,1024]{2,1,0:T(8,128)(2,1)S(1)}, u32[]{:S(2)}, u32[]{:S(2)}) %collective-permute-start.2) | collective-permute-done | bytes 131104 | tf_op jit(solution)/shard_map/ppermute | solution.py:30
  13.9 0.0 collective-permute-start.3
  13.9 1.3 %collective-permute-done.3 = bf16[4,16,1024]{2,1,0:T(8,128)(2,1)S(1)} collective-permute-done((bf16[4,16,1024]{2,1,0:T(8,128)(2,1)S(1)}, bf16[4,16,1024]{2,1,0:T(8,128)(2,1)S(1)}, u32[]{:S(2)}, u32[]{:S(2)}) %collective-permute-start.3) | collective-permute-done | bytes 131104 | tf_op jit(solution)/shard_map/ppermute | solution.py:30
  15.4 0.0 copy-start.4
  15.4 1.3 %pad_maximum_fusion = bf16[288,2048]{1,0:T(8,128)(2,1)S(1)} fusion(bf16[32,2048]{1,0:T(8,128)(2,1)S(1)} %reshape.27, bf16[256,2048]{1,0:T(8,128)(2,1)} %bitcast.refs_6_), kind=kLoop, calls=%fused_computation | loop fusion | flops 2359296 | bytes 2359296 | tf_op jit(solution)/shard_map/concatenate | solution.py:312
  16.7 3.8 %collective-permute-start.4 = (bf16[288,2048]{1,0:T(8,128)(2,1)S(1)}, bf16[288,2048]{1,0:T(8,128)(2,1)S(1)}, u32[]{:S(2)}, u32[]{:S(2)}) collective-permute-start(bf16[288,2048]{1,0:T(8,128)(2,1)S(1)} %pad_maximum_fusion), channel_id=1, source_target_pairs={{1,5},{3,7},{5,9},{7,11},{9,13},{11,15},{17,21},{19,23},{21,25},{2... | collective-permute-start | bytes 3538952 | tf_op jit(solution)/shard_map/ppermute | solution.py:30
  20.5 1.6 %collective-permute-start.10 = (bf16[256,2048]{1,0:T(8,128)(2,1)}, bf16[256,2048]{1,0:T(8,128)(2,1)}, u32[]{:S(2)}, u32[]{:S(2)}) collective-permute-start(bf16[256,2048]{1,0:T(8,128)(2,1)} %bitcast.refs_6_), channel_id=1, source_target_pairs={{0,4},{2,6},{4,8},{6,10},{8,12},{10,14},{16,20},{18,22},{20,24},{2... | collective-permute-start | bytes 3145736 | tf_op jit(solution)/shard_map/ppermute | solution.py:30
  22.2 1.6 %collective-permute-start.18 = (bf16[256,2048]{1,0:T(8,128)(2,1)}, bf16[256,2048]{1,0:T(8,128)(2,1)}, u32[]{:S(2)}, u32[]{:S(2)}) collective-permute-start(bf16[256,2048]{1,0:T(8,128)(2,1)} %bitcast.refs_6_), channel_id=1, source_target_pairs={{0,2},{2,0},{4,6},{6,4},{8,10},{10,8},{12,14},{14,12},{16,18},{18,... | collective-permute-start | bytes 3145736 | tf_op jit(solution)/shard_map/ppermute | solution.py:30
  23.8 2.3 %collective-permute-start.15 = (bf16[256,2048]{1,0:T(8,128)(2,1)}, bf16[256,2048]{1,0:T(8,128)(2,1)}, u32[]{:S(2)}, u32[]{:S(2)}) collective-permute-start(bf16[256,2048]{1,0:T(8,128)(2,1)} %bitcast.refs_6_), channel_id=1, source_target_pairs={{0,1},{1,0},{2,3},{3,2},{4,5},{5,4},{6,7},{7,6},{8,9},{9,8},{10,11... | collective-permute-start | bytes 3145736 | tf_op jit(solution)/shard_map/ppermute | solution.py:30
  26.1 2.2 %collective-permute-start.8 = (bf16[256,2048]{1,0:T(8,128)(2,1)}, bf16[256,2048]{1,0:T(8,128)(2,1)S(1)}, u32[]{:S(2)}, u32[]{:S(2)}) collective-permute-start(bf16[256,2048]{1,0:T(8,128)(2,1)} %bitcast.refs_6_), channel_id=1, source_target_pairs={{1,3},{5,7},{9,11},{13,15},{17,19},{21,23},{25,27},{29,31}} | collective-permute-start | bytes 3145736 | tf_op jit(solution)/shard_map/ppermute | solution.py:30
  28.3 0.0 collective-permute-done.10.refs_7_
  28.3 1.7 %collective-permute-start.11 = (bf16[256,2048]{1,0:T(8,128)(2,1)}, bf16[256,2048]{1,0:T(8,128)(2,1)}, u32[]{:S(2)}, u32[]{:S(2)}) collective-permute-start(bf16[256,2048]{1,0:T(8,128)(2,1)} %collective-permute-done.10.refs_7_), channel_id=1, source_target_pairs={{0,2},{2,0},{4,6},{6,4},{8,10},{10,8},{12,14},{14,12},{16,18},{18,... | collective-permute-start | bytes 3145736 | tf_op jit(solution)/shard_map/ppermute | solution.py:30
  30.0 14.6 %collective-permute-done.4 = bf16[288,2048]{1,0:T(8,128)(2,1)S(1)} collective-permute-done((bf16[288,2048]{1,0:T(8,128)(2,1)S(1)}, bf16[288,2048]{1,0:T(8,128)(2,1)S(1)}, u32[]{:S(2)}, u32[]{:S(2)}) %collective-permute-start.4) | collective-permute-done | bytes 1179680 | tf_op jit(solution)/shard_map/ppermute | solution.py:30
  44.6 4.2 %collective-permute-start.16 = (bf16[256,2048]{1,0:T(8,128)(2,1)}, bf16[256,2048]{1,0:T(8,128)(2,1)}, u32[]{:S(2)}, u32[]{:S(2)}) collective-permute-start(bf16[256,2048]{1,0:T(8,128)(2,1)} %collective-permute-done.10.refs_7_), channel_id=1, source_target_pairs={{0,1},{1,0},{2,3},{3,2},{4,5},{5,4},{6,7},{7,6},{8,9},{9,8},{10,11... | collective-permute-start | bytes 3145736 | tf_op jit(solution)/shard_map/ppermute | solution.py:30
  48.8 1.1 slice.8.refs_8_
  49.9 0.0 collective-permute-done.18.refs_9_
  49.9 4.1 %collective-permute-start.5 = (bf16[256,2048]{1,0:T(8,128)(2,1)}, bf16[256,2048]{1,0:T(8,128)(2,1)S(1)}, u32[]{:S(2)}, u32[]{:S(2)}) collective-permute-start(bf16[256,2048]{1,0:T(8,128)(2,1)} %slice.8.refs_8_), channel_id=1, source_target_pairs={{1,4},{3,6},{5,8},{7,10},{9,12},{11,14},{17,20},{19,22},{21,24},{2... | collective-permute-start | bytes 3145736 | tf_op jit(solution)/shard_map/ppermute | solution.py:30
  54.0 0.0 collective-permute-done.15.refs_0_
  54.1 0.1 collective-permute-start.14
  54.1 0.5 collective-permute-start.19
  54.6 0.8 collective-permute-done.14
  55.5 0.7 copy-done.2
  56.1 2.1 %collective-permute-start.21 = (bf16[256,2048]{1,0:T(8,128)(2,1)}, bf16[256,2048]{1,0:T(8,128)(2,1)}, u32[]{:S(2)}, u32[]{:S(2)}) collective-permute-start(bf16[256,2048]{1,0:T(8,128)(2,1)} %slice.8.refs_8_), channel_id=1, source_target_pairs={{1,3},{3,1},{5,7},{7,5},{9,11},{11,9},{13,15},{15,13},{17,19},{19,... | collective-permute-start | bytes 3145736 | tf_op jit(solution)/shard_map/ppermute | solution.py:30
  58.3 0.1 tile.4
  58.4 0.2 tile.10
  58.6 0.2 copy.17.inf
  58.8 0.0 copy-start.1
  58.8 1.3 %pad_maximum_fusion.1.gi = bf16[1024,384]{1,0:T(8,128)(2,1)S(1)} fusion(bf16[1024,128]{1,0:T(8,128)(2,1)S(1)} %convert_element_type.31, bf16[1024,256]{1,0:T(8,128)(2,1)} %param.11), kind=kLoop, calls=%fused_computation.1 | loop fusion | flops 1572864 | bytes 1572864 | tf_op jit(solution)/shard_map/concatenate | solution.py:295
  60.1 3.1 %collective-permute-start.17 = (bf16[256,2048]{1,0:T(8,128)(2,1)}, bf16[256,2048]{1,0:T(8,128)(2,1)S(1)}, u32[]{:S(2)}, u32[]{:S(2)}) collective-permute-start(bf16[256,2048]{1,0:T(8,128)(2,1)} %slice.8.refs_8_), channel_id=1, source_target_pairs={{0,1},{1,0},{2,3},{3,2},{4,5},{5,4},{6,7},{7,6},{8,9},{9,8},{10,11... | collective-permute-start | bytes 3145736 | tf_op jit(solution)/shard_map/ppermute | solution.py:30
  63.2 0.0 collective-permute-done.16.refs_1_
  63.2 0.7 collective-permute-start.12
  63.9 2.0 %collective-permute-done.5.refs_5_ = bf16[256,2048]{1,0:T(8,128)(2,1)S(1)} collective-permute-done((bf16[256,2048]{1,0:T(8,128)(2,1)}, bf16[256,2048]{1,0:T(8,128)(2,1)S(1)}, u32[]{:S(2)}, u32[]{:S(2)}) %collective-permute-start.5) | collective-permute-done | bytes 1048608 | tf_op jit(solution)/shard_map/ppermute | solution.py:30
  65.9 0.9 collective-permute-start.6
  66.9 4.7 %shard_map.82 = (bf16[1024,2048]{1,0:T(8,128)(2,1)S(1)}, f32[1024,128]{1,0:T(8,128)S(1)}, bf16[1024,1024]{1,0:T(8,128)(2,1)S(1)}) custom-call(bf16[1024,1024]{1,0:T(8,128)(2,1)S(1)} %copy-done.1, bf16[1024,384]{1,0:T(8,128)(2,1)S(1)} %pad_maximum_fusion.1.gi, f32[1024,128]{1,0:T(8,128)S(1)} %copy.17.inf, bf16[4,16,1024]{2,1,0:T(8,128)(2,1)S(1)} %pad_maximum_fusion.2.s0, ...), custom_call_target="tpu_custom_call" | custom-call | flops 4294967296 | bytes 3670016 | tf_op jit(solution)/shard_map/pallas_call | solution.py:231
  71.5 3.6 %shard_map.83 = (bf16[1024,2048]{1,0:T(8,128)(2,1)S(1)}, f32[1024,128]{1,0:T(8,128)S(1)}, bf16[1024,1024]{1,0:T(8,128)(2,1)S(1)}) custom-call(bf16[1024,1024]{1,0:T(8,128)(2,1)S(1)} %copy-done.1, bf16[1024,384]{1,0:T(8,128)(2,1)S(1)} %pad_maximum_fusion.1.gi, ...), custom_call_target="tpu_custom_call", output_to_operand_aliasing={{0}: (5, {}), {1}: (6, {})} | custom-call | flops 3221225472 | bytes 9961472 | tf_op jit(solution)/shard_map/pallas_call | solution.py:231
  75.1 0.0 collective-permute-done.19.refs_3_
  75.1 3.4 %collective-permute-start.20 = (bf16[256,2048]{1,0:T(8,128)(2,1)}, bf16[256,2048]{1,0:T(8,128)(2,1)S(1)}, u32[]{:S(2)}, u32[]{:S(2)}) collective-permute-start(bf16[256,2048]{1,0:T(8,128)(2,1)} %collective-permute-done.11.refs_10_), channel_id=1, source_target_pairs={{0,1},{1,0},{2,3},{3,2},{4,5},{5,4},{6,7},{7,6},{8,9},{9,8},{10,11... | collective-permute-start | bytes 3145736 | tf_op jit(solution)/shard_map/ppermute | solution.py:30
  78.5 0.1 collective-permute-start.22
  78.6 3.6 %shard_map.84 = (bf16[1024,2048]{1,0:T(8,128)(2,1)S(1)}, f32[1024,128]{1,0:T(8,128)S(1)}, bf16[1024,1024]{1,0:T(8,128)(2,1)S(1)}) custom-call(bf16[1024,1024]{1,0:T(8,128)(2,1)S(1)} %copy-done.1, bf16[1024,384]{1,0:T(8,128)(2,1)S(1)} %pad_maximum_fusion.1.gi, ...), custom_call_target="tpu_custom_call", output_to_operand_aliasing={{0}: (5, {}), {1}: (6, {})} | custom-call | flops 3221225472 | bytes 9961472 | tf_op jit(solution)/shard_map/pallas_call | solution.py:231
  82.2 0.5 collective-permute-start.9
  82.7 0.1 collective-permute-start.13
  82.8 0.0 collective-permute-done.6.refs_3_
  82.8 2.6 %collective-permute-start.7 = (bf16[256,2048]{1,0:T(8,128)(2,1)S(1)}, bf16[256,2048]{1,0:T(8,128)(2,1)S(1)}, u32[]{:S(2)}, u32[]{:S(2)}) collective-permute-start(bf16[256,2048]{1,0:T(8,128)(2,1)S(1)} %collective-permute-done.6.refs_3_), channel_id=1, source_target_pairs={{0,1},{1,0},{2,3},{3,2},{4,5},{5,4},{6,7},{7,6},{8,9},{9,8},{10,11... | collective-permute-start | bytes 3145736 | tf_op jit(solution)/shard_map/ppermute | solution.py:30
  85.4 5.4 %shard_map.85 = (bf16[1024,256]{1,0:T(8,128)(2,1)S(1)}, bf16[1024,256]{1,0:T(8,128)(2,1)S(1)}, bf16[1024,256]{1,0:T(8,128)(2,1)S(1)}, bf16[1024,128]{1,0:T(8,128)(2,1)S(1)}) custom-call(bf16[1024,1024]{1,0:T(8,128)(2,1)S(1)} %copy-done.1, bf16[1024,384]{1,0:T(8,128)(2,1)S(1)} %pad_maximum_fusion.1.gi, bf16[4,16,1024]{2,1,0:T(8,128)(2,1)S(1)} %pad_maximum_fusion.2.s0, ...), custom_call_target="tpu_custom_call" | custom-call | flops 4831838208 | bytes 3276800 | tf_op jit(solution)/shard_map/pallas_call | solution.py:231
  90.8 0.2 shard_map.87.refs_14_
  91.1 2.3 %shard_map.86 = (bf16[1024,2048]{1,0:T(8,128)(2,1)S(1)}, bf16[1024,128]{1,0:T(8,128)(2,1)S(1)}) custom-call(bf16[1024,1024]{1,0:T(8,128)(2,1)S(1)} %get-tuple-element.26.p, bf16[1024,256]{1,0:T(8,128)(2,1)S(1)} %get-tuple-element.27.f5, bf16[1024,256]{1,0:T(8,128)(2,1)S(1)} %get-tuple-element.28.f6, ...), custom_call_target="tpu_custom_call", output_to_operand_aliasing={{0}: (5, {})} | custom-call | flops 2147483648 | bytes 8650752 | tf_op jit(solution)/shard_map/pallas_call | solution.py:231
  93.4 0.0 collective-permute-done.20.refs_4_
  93.4 11.3 %shard_map.88.refs_8_ = f32[1024,2048]{1,0:T(8,128)} custom-call(bf16[256,2048]{1,0:T(8,128)(2,1)} %collective-permute-done.15.refs_0_, bf16[256,2048]{1,0:T(8,128)(2,1)} %collective-permute-done.16.refs_1_, bf16[256,2048]{1,0:T(8,128)(2,1)S(1)} %collective-permute-done.17.refs_2_, bf16[256,2048]{1,0:T(8,128)(2,1)} %collective-permute-done.19.refs_3_, ...), custom_call_target="tpu_custom_call" | custom-call | flops 7516192768 | bytes 16777216 | tf_op jit(solution)/shard_map/pallas_call | solution.py:253
  104.8 0.0 collective-permute-done.9.refs_1_
  104.8 0.0 collective-permute-done.13.refs_2_
  104.8 0.0 copy-start
  104.8 3.4 %copy-done = f32[1024,2048]{1,0:T(8,128)S(1)} copy-done((f32[1024,2048]{1,0:T(8,128)S(1)}, f32[1024,2048]{1,0:T(8,128)}, u32[]{:S(2)}) %copy-start) | copy-done | bytes 8388632
  108.2 5.6 %shard_map.89 = f32[1024,2048]{1,0:T(8,128)} custom-call(bf16[256,2048]{1,0:T(8,128)(2,1)S(1)} %collective-permute-done.7.refs_0_, bf16[256,2048]{1,0:T(8,128)(2,1)S(1)} %collective-permute-done.9.refs_1_, bf16[256,2048]{1,0:T(8,128)(2,1)S(1)} %collective-permute-done.13.refs_2_, bf16[256,2048]{1,0:T(8,128)(2,1)S(1)} %collective-permute-done.6.refs_3_, ...), custom_call_target="tpu_custom_call" | custom-call | flops 3221225472 | bytes 16777216 | tf_op jit(solution)/shard_map/pallas_call | solution.py:253
  (25 shorter events, 0.3 us)
Async XLA Ops:
  3.2 1.3 %collective-permute-start = (bf16[1,16,1024]{2,1,0:T(8,128)(2,1)S(1)}, bf16[1,16,1024]{2,1,0:T(8,128)(2,1)S(1)}, u32[]{:S(2)}, u32[]{:S(2)}) collective-permute-start(bf16[1,16,1024]{2,1,0:T(8,128)(2,1)S(1)} %bitcast.9), channel_id=1, source_target_pairs={{0,1},{1,0},{2,3},{3,2},{4,5},{5,4},{6,7},{7,6},{8,9},{9,8},{10,11... | collective-permute-start | bytes 98312 | tf_op jit(solution)/shard_map/ppermute | solution.py:30
  4.5 4.6 %collective-permute-start.1 = (bf16[2,16,1024]{2,1,0:T(8,128)(2,1)S(1)}, bf16[2,16,1024]{2,1,0:T(8,128)(2,1)S(1)}, u32[]{:S(2)}, u32[]{:S(2)}) collective-permute-start(bf16[2,16,1024]{2,1,0:T(8,128)(2,1)S(1)} %pad_maximum_fusion.3), channel_id=1, source_target_pairs={{0,2},{2,0},{1,3},{3,1},{4,6},{6,4},{5,7},{7,5},{8,10},{10,8},{9,1... | collective-permute-start | bytes 196616 | tf_op jit(solution)/shard_map/ppermute | solution.py:30
  9.0 4.9 %collective-permute-start.2 = (bf16[4,16,1024]{2,1,0:T(8,128)(2,1)S(1)}, bf16[4,16,1024]{2,1,0:T(8,128)(2,1)S(1)}, u32[]{:S(2)}, u32[]{:S(2)}) collective-permute-start(bf16[4,16,1024]{2,1,0:T(8,128)(2,1)S(1)} %pad_maximum_fusion.2.s0), channel_id=1, source_target_pairs={{1,5},{3,7},{5,9},{7,11},{9,13},{11,15},{17,21},{19,23},{21,25},{2... | collective-permute-start | bytes 393224 | tf_op jit(solution)/shard_map/ppermute | solution.py:30
  13.9 1.3 %collective-permute-start.3 = (bf16[4,16,1024]{2,1,0:T(8,128)(2,1)S(1)}, bf16[4,16,1024]{2,1,0:T(8,128)(2,1)S(1)}, u32[]{:S(2)}, u32[]{:S(2)}) collective-permute-start(bf16[4,16,1024]{2,1,0:T(8,128)(2,1)S(1)} %collective-permute-done.2), channel_id=1, source_target_pairs={{0,1},{1,0},{2,3},{3,2},{4,5},{5,4},{6,7},{7,6},{8,9},{9,8},{10,11... | collective-permute-start | bytes 393224 | tf_op jit(solution)/shard_map/ppermute | solution.py:30
  15.4 42.9 %copy-start.4 = (f32[1024,4]{0,1:T(4,128)S(1)}, f32[1024,4]{0,1:T(4,128)}, u32[]{:S(2)}) copy-start(f32[1024,4]{0,1:T(4,128)} %param.13) | copy-start | bytes 49156
  16.7 27.9 %collective-permute-start.4 = (bf16[288,2048]{1,0:T(8,128)(2,1)S(1)}, bf16[288,2048]{1,0:T(8,128)(2,1)S(1)}, u32[]{:S(2)}, u32[]{:S(2)}) collective-permute-start(bf16[288,2048]{1,0:T(8,128)(2,1)S(1)} %pad_maximum_fusion), channel_id=1, source_target_pairs={{1,5},{3,7},{5,9},{7,11},{9,13},{11,15},{17,21},{19,23},{21,25},{2... | collective-permute-start | bytes 3538952 | tf_op jit(solution)/shard_map/ppermute | solution.py:30
  20.5 7.8 %collective-permute-start.10 = (bf16[256,2048]{1,0:T(8,128)(2,1)}, bf16[256,2048]{1,0:T(8,128)(2,1)}, u32[]{:S(2)}, u32[]{:S(2)}) collective-permute-start(bf16[256,2048]{1,0:T(8,128)(2,1)} %bitcast.refs_6_), channel_id=1, source_target_pairs={{0,4},{2,6},{4,8},{6,10},{8,12},{10,14},{16,20},{18,22},{20,24},{2... | collective-permute-start | bytes 3145736 | tf_op jit(solution)/shard_map/ppermute | solution.py:30
  22.2 27.7 %collective-permute-start.18 = (bf16[256,2048]{1,0:T(8,128)(2,1)}, bf16[256,2048]{1,0:T(8,128)(2,1)}, u32[]{:S(2)}, u32[]{:S(2)}) collective-permute-start(bf16[256,2048]{1,0:T(8,128)(2,1)} %bitcast.refs_6_), channel_id=1, source_target_pairs={{0,2},{2,0},{4,6},{6,4},{8,10},{10,8},{12,14},{14,12},{16,18},{18,... | collective-permute-start | bytes 3145736 | tf_op jit(solution)/shard_map/ppermute | solution.py:30
  23.8 30.2 %collective-permute-start.15 = (bf16[256,2048]{1,0:T(8,128)(2,1)}, bf16[256,2048]{1,0:T(8,128)(2,1)}, u32[]{:S(2)}, u32[]{:S(2)}) collective-permute-start(bf16[256,2048]{1,0:T(8,128)(2,1)} %bitcast.refs_6_), channel_id=1, source_target_pairs={{0,1},{1,0},{2,3},{3,2},{4,5},{5,4},{6,7},{7,6},{8,9},{9,8},{10,11... | collective-permute-start | bytes 3145736 | tf_op jit(solution)/shard_map/ppermute | solution.py:30
  26.1 28.0 %collective-permute-start.8 = (bf16[256,2048]{1,0:T(8,128)(2,1)}, bf16[256,2048]{1,0:T(8,128)(2,1)S(1)}, u32[]{:S(2)}, u32[]{:S(2)}) collective-permute-start(bf16[256,2048]{1,0:T(8,128)(2,1)} %bitcast.refs_6_), channel_id=1, source_target_pairs={{1,3},{5,7},{9,11},{13,15},{17,19},{21,23},{25,27},{29,31}} | collective-permute-start | bytes 3145736 | tf_op jit(solution)/shard_map/ppermute | solution.py:30
  28.3 31.8 %collective-permute-start.11 = (bf16[256,2048]{1,0:T(8,128)(2,1)}, bf16[256,2048]{1,0:T(8,128)(2,1)}, u32[]{:S(2)}, u32[]{:S(2)}) collective-permute-start(bf16[256,2048]{1,0:T(8,128)(2,1)} %collective-permute-done.10.refs_7_), channel_id=1, source_target_pairs={{0,2},{2,0},{4,6},{6,4},{8,10},{10,8},{12,14},{14,12},{16,18},{18,... | collective-permute-start | bytes 3145736 | tf_op jit(solution)/shard_map/ppermute | solution.py:30
  44.6 18.6 %collective-permute-start.16 = (bf16[256,2048]{1,0:T(8,128)(2,1)}, bf16[256,2048]{1,0:T(8,128)(2,1)}, u32[]{:S(2)}, u32[]{:S(2)}) collective-permute-start(bf16[256,2048]{1,0:T(8,128)(2,1)} %collective-permute-done.10.refs_7_), channel_id=1, source_target_pairs={{0,1},{1,0},{2,3},{3,2},{4,5},{5,4},{6,7},{7,6},{8,9},{9,8},{10,11... | collective-permute-start | bytes 3145736 | tf_op jit(solution)/shard_map/ppermute | solution.py:30
  49.9 16.0 %collective-permute-start.5 = (bf16[256,2048]{1,0:T(8,128)(2,1)}, bf16[256,2048]{1,0:T(8,128)(2,1)S(1)}, u32[]{:S(2)}, u32[]{:S(2)}) collective-permute-start(bf16[256,2048]{1,0:T(8,128)(2,1)} %slice.8.refs_8_), channel_id=1, source_target_pairs={{1,4},{3,6},{5,8},{7,10},{9,12},{11,14},{17,20},{19,22},{21,24},{2... | collective-permute-start | bytes 3145736 | tf_op jit(solution)/shard_map/ppermute | solution.py:30
  54.1 1.4 %collective-permute-start.14 = (bf16[4,16,1024]{2,1,0:T(8,128)(2,1)S(1)}, bf16[4,16,1024]{2,1,0:T(8,128)(2,1)S(1)}, u32[]{:S(2)}, u32[]{:S(2)}) collective-permute-start(bf16[4,16,1024]{2,1,0:T(8,128)(2,1)S(1)} %reshape.28), channel_id=1, source_target_pairs={{0,1},{1,0},{2,3},{3,2},{4,5},{5,4},{6,7},{7,6},{8,9},{9,8},{10,11... | collective-permute-start | bytes 393224 | tf_op jit(solution)/shard_map/ppermute | solution.py:30
  54.1 21.0 %collective-permute-start.19 = (bf16[256,2048]{1,0:T(8,128)(2,1)}, bf16[256,2048]{1,0:T(8,128)(2,1)}, u32[]{:S(2)}, u32[]{:S(2)}) collective-permute-start(bf16[256,2048]{1,0:T(8,128)(2,1)} %collective-permute-done.18.refs_9_), channel_id=1, source_target_pairs={{0,1},{1,0},{2,3},{3,2},{4,5},{5,4},{6,7},{7,6},{8,9},{9,8},{10,11... | collective-permute-start | bytes 3145736 | tf_op jit(solution)/shard_map/ppermute | solution.py:30
  55.5 0.7 copy-start.2
  56.1 22.4 %collective-permute-start.21 = (bf16[256,2048]{1,0:T(8,128)(2,1)}, bf16[256,2048]{1,0:T(8,128)(2,1)}, u32[]{:S(2)}, u32[]{:S(2)}) collective-permute-start(bf16[256,2048]{1,0:T(8,128)(2,1)} %slice.8.refs_8_), channel_id=1, source_target_pairs={{1,3},{3,1},{5,7},{7,5},{9,11},{11,9},{13,15},{15,13},{17,19},{19,... | collective-permute-start | bytes 3145736 | tf_op jit(solution)/shard_map/ppermute | solution.py:30
  58.8 8.1 %copy-start.1 = (bf16[1024,1024]{1,0:T(8,128)(2,1)S(1)}, bf16[1024,1024]{1,0:T(8,128)(2,1)}, u32[]{:S(2)}) copy-start(bf16[1024,1024]{1,0:T(8,128)(2,1)} %c.7) | copy-start | bytes 6291460
  60.1 22.1 %collective-permute-start.17 = (bf16[256,2048]{1,0:T(8,128)(2,1)}, bf16[256,2048]{1,0:T(8,128)(2,1)S(1)}, u32[]{:S(2)}, u32[]{:S(2)}) collective-permute-start(bf16[256,2048]{1,0:T(8,128)(2,1)} %slice.8.refs_8_), channel_id=1, source_target_pairs={{0,1},{1,0},{2,3},{3,2},{4,5},{5,4},{6,7},{7,6},{8,9},{9,8},{10,11... | collective-permute-start | bytes 3145736 | tf_op jit(solution)/shard_map/ppermute | solution.py:30
  63.2 19.5 %collective-permute-start.12 = (bf16[256,2048]{1,0:T(8,128)(2,1)}, bf16[256,2048]{1,0:T(8,128)(2,1)S(1)}, u32[]{:S(2)}, u32[]{:S(2)}) collective-permute-start(bf16[256,2048]{1,0:T(8,128)(2,1)} %collective-permute-done.11.refs_10_), channel_id=1, source_target_pairs={{0,5},{4,9},{8,13},{16,21},{20,25},{24,29}} | collective-permute-start | bytes 3145736 | tf_op jit(solution)/shard_map/ppermute | solution.py:30
  65.9 16.9 %collective-permute-start.6 = (bf16[256,2048]{1,0:T(8,128)(2,1)S(1)}, bf16[256,2048]{1,0:T(8,128)(2,1)S(1)}, u32[]{:S(2)}, u32[]{:S(2)}) collective-permute-start(bf16[256,2048]{1,0:T(8,128)(2,1)S(1)} %collective-permute-done.5.refs_5_), channel_id=1, source_target_pairs={{2,0},{6,4},{10,8},{14,12},{18,16},{22,20},{26,24},{30,28}} | collective-permute-start | bytes 3145736 | tf_op jit(solution)/shard_map/ppermute | solution.py:30
  75.1 18.3 %collective-permute-start.20 = (bf16[256,2048]{1,0:T(8,128)(2,1)}, bf16[256,2048]{1,0:T(8,128)(2,1)S(1)}, u32[]{:S(2)}, u32[]{:S(2)}) collective-permute-start(bf16[256,2048]{1,0:T(8,128)(2,1)} %collective-permute-done.11.refs_10_), channel_id=1, source_target_pairs={{0,1},{1,0},{2,3},{3,2},{4,5},{5,4},{6,7},{7,6},{8,9},{9,8},{10,11... | collective-permute-start | bytes 3145736 | tf_op jit(solution)/shard_map/ppermute | solution.py:30
  78.5 14.9 %collective-permute-start.22 = (bf16[256,2048]{1,0:T(8,128)(2,1)}, bf16[256,2048]{1,0:T(8,128)(2,1)S(1)}, u32[]{:S(2)}, u32[]{:S(2)}) collective-permute-start(bf16[256,2048]{1,0:T(8,128)(2,1)} %collective-permute-done.21.refs_11_), channel_id=1, source_target_pairs={{0,1},{1,0},{2,3},{3,2},{4,5},{5,4},{6,7},{7,6},{8,9},{9,8},{10,11... | collective-permute-start | bytes 3145736 | tf_op jit(solution)/shard_map/ppermute | solution.py:30
  78.6 3.6 %copy-start.3 = (bf16[4,16,1024]{2,1,0:T(8,128)(2,1)S(1)}, bf16[4,16,1024]{2,1,0:T(8,128)(2,1)}, u32[]{:S(2)}) copy-start(bf16[4,16,1024]{2,1,0:T(8,128)(2,1)} %copy-done.2) | copy-start | bytes 393220
  82.2 22.6 %collective-permute-start.9 = (bf16[256,2048]{1,0:T(8,128)(2,1)S(1)}, bf16[256,2048]{1,0:T(8,128)(2,1)S(1)}, u32[]{:S(2)}, u32[]{:S(2)}) collective-permute-start(bf16[256,2048]{1,0:T(8,128)(2,1)S(1)} %collective-permute-done.8.refs_4_), channel_id=1, source_target_pairs={{0,1},{1,0},{2,3},{3,2},{4,5},{5,4},{6,7},{7,6},{8,9},{9,8},{10,11... | collective-permute-start | bytes 3145736 | tf_op jit(solution)/shard_map/ppermute | solution.py:30
  82.7 22.1 %collective-permute-start.13 = (bf16[256,2048]{1,0:T(8,128)(2,1)S(1)}, bf16[256,2048]{1,0:T(8,128)(2,1)S(1)}, u32[]{:S(2)}, u32[]{:S(2)}) collective-permute-start(bf16[256,2048]{1,0:T(8,128)(2,1)S(1)} %collective-permute-done.12.refs_6_), channel_id=1, source_target_pairs={{0,1},{1,0},{2,3},{3,2},{4,5},{5,4},{6,7},{7,6},{8,9},{9,8},{10,11... | collective-permute-start | bytes 3145736 | tf_op jit(solution)/shard_map/ppermute | solution.py:30
  82.8 22.0 %collective-permute-start.7 = (bf16[256,2048]{1,0:T(8,128)(2,1)S(1)}, bf16[256,2048]{1,0:T(8,128)(2,1)S(1)}, u32[]{:S(2)}, u32[]{:S(2)}) collective-permute-start(bf16[256,2048]{1,0:T(8,128)(2,1)S(1)} %collective-permute-done.6.refs_3_), channel_id=1, source_target_pairs={{0,1},{1,0},{2,3},{3,2},{4,5},{5,4},{6,7},{7,6},{8,9},{9,8},{10,11... | collective-permute-start | bytes 3145736 | tf_op jit(solution)/shard_map/ppermute | solution.py:30
  104.8 3.4 %copy-start = (f32[1024,2048]{1,0:T(8,128)S(1)}, f32[1024,2048]{1,0:T(8,128)}, u32[]{:S(2)}) copy-start(f32[1024,2048]{1,0:T(8,128)} %shard_map.88.refs_8_) | copy-start | bytes 25165828

commit v2 on v0

v2 whole, which is shorter than its diff:
```python
import functools

import jax
import jax.numpy as jnp
from jax import lax
from jax.experimental import pallas as pl
from jax.experimental.pallas import tpu as pltpu
from jax.sharding import PartitionSpec as P

MIB = 1 << 20
LIMIT = 20 * MIB
VMEM = pl.BlockSpec(memory_space=pltpu.VMEM)
ANY = pl.BlockSpec(memory_space=pl.ANY)
F32 = jnp.float32
BF16 = jnp.bfloat16
LAGS = 8
COLS = 256
ROWS = 8


def position():
    return lax.rem(lax.axis_index("tm"), 4)


def send(block, pairs):
    count = lax.axis_size("tm")
    route = []
    for level in range(count // 4):
        for a, b, step in pairs:
            if level + step < count // 4:
                route.append((level * 4 + a, (level + step) * 4 + b))
    return lax.ppermute(block, "tm", route)


def after(block, *others):
    return lax.optimization_barrier((block, *others))[0]


CORE = [(0, 1, 0), (1, 0, 0), (2, 3, 0), (3, 2, 0)]
ROW = [(0, 2, 0), (2, 0, 0), (1, 3, 0), (3, 1, 0)]
ROW0 = [(0, 2, 0), (2, 0, 0)]
ALL = [(0, 0, 1), (1, 1, 1), (2, 2, 1), (3, 3, 1)]
ROW1 = [(1, 3, 0), (3, 1, 0)]


def record_of(j, lag, near, far=None, swapped=None):
    d = j - lag
    pos = lax.rem(d + 8, 4)
    row = jnp.where(d >= 0, near[0, pos ^ (j | 1)], near[1, pos ^ (j | 1)])
    if far is not None:
        held = jnp.where((j & 1) == 0, far[pos ^ (j | 1)], swapped[pos ^ (j | 1)])
        row = jnp.where(d >= -4, row, held)
    return row.astype(F32)


def call(kernel, outs, ins, scratch=(), flops=0, spec=VMEM, limit=LIMIT):
    moved = sum(a.size * a.dtype.itemsize for a in ins)
    return pl.pallas_call(
        kernel,
        out_shape=outs,
        in_specs=[spec] * len(ins),
        out_specs=[VMEM] * len(outs),
        scratch_shapes=list(scratch),
        cost_estimate=pl.CostEstimate(flops=flops, bytes_accessed=moved, transcendentals=0),
        compiler_params=pltpu.CompilerParams(vmem_limit_bytes=limit),
    )(*ins)


def build(c_ref, rec, t_ref):
    width = t_ref.shape[0]
    size = width // 8
    eye = (
        lax.broadcasted_iota(jnp.int32, (size, size), 0)
        == lax.broadcasted_iota(jnp.int32, (size, size), 1)
    ).astype(F32)
    for p in range(8):
        rows = slice(p * size, (p + 1) * size)
        half = p % 2 * width
        masked = c_ref[rows, :].astype(F32) * rec[p // 2 : p // 2 + 1, half : half + width]
        t_ref[rows, :] = masked.astype(BF16)
        rate = rec[4:5, p * size : (p + 1) * size]
        t_ref[rows, rows] = (masked[:, rows] + eye * rate).astype(BF16)


def times(left, right):
    return jnp.dot(left, right, preferred_element_type=F32)


def split(value, m, w):
    sens = m.shape[1]
    m[...] = value[:, :sens].astype(BF16)
    w[...] = value[:, sens:]


def record_kernel(decay, mask, lanes, load, out, *scratch):
    held, sems = scratch[:4], scratch[4]
    moves = [
        pltpu.make_async_copy(source, target, sems.at[i])
        for i, (source, target) in enumerate(zip((decay, mask, lanes, load), held))
    ]
    for move in moves:
        move.start()
    for move in moves:
        move.wait()
    decay, mask, lanes, load = held
    width = decay.shape[1]
    size = width // 8
    flags = mask[...]
    for q in range(8):
        wide = jnp.broadcast_to(flags[0, :, q : q + 1].astype(F32), (8, size)).astype(BF16)
        for p in range(8):
            first = p % 2 * width + q * size
            out[0, p // 2 : p // 2 + 1, first : first + size] = wide[p : p + 1]
    rate = decay[...]
    loads = load[...]
    high = loads.astype(BF16).astype(F32)
    rows = [jnp.concatenate([rate, jnp.zeros_like(rate)], axis=1)]
    rows += [lanes[...].astype(F32), high, loads - high]
    out[0, 4:, :] = jnp.concatenate(rows, axis=0).astype(BF16)


def load_kernel(c, gain, inf, c_out, gi, spread, inf_held, sems):
    sens = gain.shape[1]
    moves = [
        pltpu.make_async_copy(c, c_out, sems.at[0]),
        pltpu.make_async_copy(gain, gi.at[:, :sens], sems.at[1]),
        pltpu.make_async_copy(inf, inf_held, sems.at[2]),
    ]
    for move in moves:
        move.start()
    moves[2].wait()
    lanes = inf_held[...]
    wide = jnp.concatenate([lanes] * (128 // lanes.shape[0]), axis=0).T
    spread[...] = wide
    gi[:, sens:] = wide.astype(BF16)
    moves[1].wait()
    moves[0].wait()


def extend(p_ref, t, q_ref):
    for n in range(0, t.shape[0], 256):
        q_ref[:, n : n + 256] = times(p_ref[...], t[:, n : n + 256]).astype(BF16)


def lag_group(shape):
    return (lax.broadcasted_iota(jnp.int32, shape, 1) & 31) >> 2


def weigh(p, gi, m, w, lag):
    sens = gi.shape[1] - 128
    value = times(p[...], gi[...])
    place = lag % 4 * sens
    m[:, place : place + sens] = value[:, :sens].astype(BF16)
    w[...] = jnp.where(lag_group(w.shape) == lag, value[:, sens:], w[...])


def first_kernel(near, c, gi, spread, q, m, w, t, p):
    sens = gi.shape[1] - 128
    j = position()
    build(c, record_of(j, 0, near), p)
    m[:, :sens] = gi[:, :sens]
    w[...] = spread[...]
    weigh(p, gi, m, w, 1)
    build(c, record_of(j, 1, near), t)
    extend(p, t, q)
    weigh(q, gi, m, w, 2)


def second_kernel(near, c, gi, p, m_in, w_in, q, m, w, t):
    sens = gi.shape[1] - 128
    build(c, record_of(position(), 2, near), t)
    m[:, : 3 * sens] = m_in[...]
    w[...] = w_in[...]
    extend(p, t, q)
    weigh(q, gi, m, w, 3)


def far_kernel(near, far, swapped, c, gi, f, fw, picks, t):
    sens = f.shape[1] // 3
    j = position()
    group = lag_group(fw.shape)
    f5, f6, f7 = (f.at[:, n * sens : (n + 1) * sens] for n in range(3))
    for lag in (6, 5, 4):
        build(c, record_of(j, lag, near, far, swapped), t)
        gain, spread = gi[:, :sens], gi[:, sens:]
        f7[...] = times(t[...], gain if lag == 6 else f7[...]).astype(BF16)
        if lag < 6:
            f6[...] = times(t[...], gain if lag == 5 else f6[...]).astype(BF16)
        if lag < 5:
            f5[...] = times(t[...], gain).astype(BF16)
        loads = spread if lag == 6 else jnp.where(group > lag + 1, fw[...], spread)
        fw[...] = times(t[...], loads).astype(BF16)
    fw[...] = jnp.where(group > 4, fw[...], gi[:, sens:])
    which = lax.broadcasted_iota(jnp.int32, (4, picks.shape[1]), 0).astype(F32)
    rows = [[], []]
    for lag in range(LAGS):
        rec = record_of(j, lag, near, far, swapped)
        mine = which == rec[5:6, :]
        for part in range(2):
            rows[part].append(jnp.where(mine, rec[6 + part : 7 + part, :], 0.0))
    high, low = (jnp.concatenate(r, axis=0).astype(BF16) for r in rows)
    for n, part in enumerate((high, low, high, jnp.zeros_like(low))):
        picks[32 * n : 32 * n + 32, :] = part


def near_kernel(near, c, gi, p, w_in, f, fw, m, t, q):
    sens = gi.shape[1] - 128
    build(c, record_of(position(), 3, near), t)
    extend(p, t, q)
    m[:, :sens] = times(q[...], gi[:, :sens]).astype(BF16)
    for n in range(3):
        right = f[:, n * sens : (n + 1) * sens]
        m[:, (n + 1) * sens : (n + 2) * sens] = times(q[...], right).astype(BF16)
    lanes = lax.broadcasted_iota(jnp.int32, w_in.shape, 1)
    full = jnp.where(lag_group(w_in.shape) > 3, times(q[...], fw[...]), w_in[...])
    high = full.astype(BF16)
    low = (full - high.astype(F32)).astype(BF16)
    m[:, 4 * sens :] = jnp.where(
        lanes < 64, high, jnp.where(lanes < 96, low, jnp.zeros_like(low))
    )


TABLE = {
    0: ["O", "CYR2", "YR1", "CR2", "R1", "Y6", "CZ3", "Z2"],
    1: ["O", "CO", "YR2", "CYR1", "R2", "CR1", "CY6", "Z3"],
    2: ["O", "CYO2", "YO1", "CR2", "R1", "CYR2", "YR1", "Z2"],
    3: ["O", "CO", "YO2", "CYO1", "R2", "CR1", "YR2", "CYR1"],
}


def sum_kernel(names, cols, *refs):
    blocks = dict(zip(names, refs[: len(names)]))
    close, distant, picks, out, outgoing, sems = refs[len(names) :]
    steps = out.shape[-1] // cols
    j = position()

    def columns(i):
        return pl.ds(pl.multiple_of(i * cols, cols), cols)

    def result(i, slot):
        return pltpu.make_async_copy(
            outgoing.at[slot], out.at[0, :, columns(i)], sems.at[slot]
        )

    for pos, held in TABLE.items():

        @pl.when(j == pos)
        def _(held=held):
            @pl.loop(0, steps)
            def _(i):
                now = lax.rem(i, 2)
                readings = [blocks[name][:, columns(i)] for name in held]
                total = times(close[...], jnp.concatenate(readings[:4], axis=0))
                rest = jnp.concatenate(readings[4:] + [picks[:, columns(i)]], axis=0)
                total += times(distant[...], rest)

                @pl.when(i >= 2)
                def _():
                    result(i - 2, now).wait()

                outgoing[now] = total
                result(i, now).start()

            for i in range(max(steps - 2, 0), steps):
                result(i, i % 2).wait()


def call_sum(blocks, close, distant, picks):
    names = sorted({name for held in TABLE.values() for name in held})
    width, scen = close.shape[0], picks.shape[1]
    cols = COLS
    return pl.pallas_call(
        functools.partial(sum_kernel, names, cols),
        out_shape=jax.ShapeDtypeStruct((1, width, scen), F32),
        in_specs=[VMEM] * (len(names) + 3),
        out_specs=ANY,
        scratch_shapes=[pltpu.VMEM((2, width, cols), F32), pltpu.SemaphoreType.DMA((2,))],
        cost_estimate=pl.CostEstimate(
            flops=2 * width * scen * (close.shape[1] + distant.shape[1]),
            bytes_accessed=16 * MIB,
            transcendentals=0,
        ),
        compiler_params=pltpu.CompilerParams(vmem_limit_bytes=LIMIT),
    )(*[blocks[n] for n in names], close, distant, picks)


def per_device(coupling, decay, block_mask, gain, readings, influence, lanes, axle_load):
    width, sens = gain.shape
    scen = readings.shape[2]
    core = lax.rem(lax.axis_index("tm"), 2)
    own = readings[0]
    shape = jax.ShapeDtypeStruct
    loads = shape((width, 128), F32)
    square = shape((width, width), BF16)
    unit = 2 * width * width * 256
    t_scratch = pltpu.VMEM((width, width), BF16)

    small = [decay, block_mask, lanes, axle_load]
    (record,) = call(
        record_kernel, [shape((1, ROWS, scen), BF16)], small,
        [pltpu.VMEM(a.shape, a.dtype) for a in small] + [pltpu.SemaphoreType.DMA((4,))],
        flops=MIB, spec=ANY, limit=56 * MIB,
    )
    r = {"O": own}
    r["R1"] = send(own, [(0, 0, 1), (2, 2, 1)])
    r["YO1"] = send(own, ROW0)
    r["CO"] = send(own, CORE)
    pair = jnp.concatenate([record, send(record, CORE)], axis=0)
    pairs = jnp.stack([pair, send(pair, [(1, 1, 1), (3, 3, 1)])])
    c, gi, spread = call(
        load_kernel, [square, shape((width, sens + 128), BF16), loads],
        [coupling, gain, influence.T],
        [pltpu.VMEM(influence.T.shape, F32), pltpu.SemaphoreType.DMA((3,))],
        flops=MIB, spec=ANY,
    )
    near = jnp.concatenate([pairs, send(pairs, ROW1)], axis=1)
    near = jnp.where(core == 1, near, send(near, CORE))
    near, r["R1"], r["YO1"], c = lax.optimization_barrier((near, r["R1"], r["YO1"], c))
    r["R2"] = send(after(own, pairs), [(1, 1, 1), (3, 3, 1)])
    far = send(near[1], [(0, 0, 1), (2, 2, 1)])
    far = (far, send(far, CORE))
    r1 = r["R1"]
    r["YR1"] = send(r1, ROW0)
    p2, close, w = call(
        first_kernel, [square, shape((width, 3 * sens), BF16), loads],
        [near, c, gi, spread], [t_scratch, t_scratch], flops=8 * unit,
    )
    p2, r2 = lax.optimization_barrier((p2, r["R2"]))
    r["R2"] = r2
    r["YR2"] = send(r2, ROW1)
    r["Z2"] = send(r2, [(1, 0, 1), (3, 2, 1)])
    r["CR2"] = send(r2, CORE)
    r["CR1"] = send(after(r1, p2), CORE)
    r["CYO1"] = send(after(r["YO1"], p2), CORE)
    p3, close, w = call(
        second_kernel, [square, shape((width, 4 * sens), BF16), loads],
        [near, c, gi, p2, close, w], [t_scratch], flops=6 * unit,
    )
    yr1 = r["YR1"] = after(r["YR1"], p3)
    r["Z3"] = send(yr1, [(0, 1, 1)])
    r["CYR1"] = send(yr1, CORE)
    far, r["CO"], r["CYO1"], r["CR1"], r["Z2"] = lax.optimization_barrier(
        (far, r["CO"], r["CYO1"], r["CR1"], r["Z2"], p3)
    )[:5]
    r["Y6"] = send(r["Z2"], [(2, 0, 0)])
    r["YO2"] = send(after(own, r["Z2"]), [(1, 3, 0)])
    f, fw, picks = call(
        far_kernel,
        [shape((width, 3 * sens), BF16), shape((width, 128), BF16), shape((128, scen), BF16)],
        [near, *far, c, gi], [t_scratch], flops=9 * unit,
    )
    p3, r["CYR1"], r["CR2"] = lax.optimization_barrier((p3, r["CYR1"], r["CR2"], f))[:3]
    r["CYR2"] = send(r["YR2"], CORE)
    (distant,) = call(
        near_kernel, [shape((width, 4 * sens + 128), BF16)],
        [near, c, gi, p3, w, f, fw], [t_scratch, t_scratch], flops=unit,
    )
    r["CZ3"] = send(after(r["Z3"], distant), CORE)
    r["CYO2"] = send(after(r["YO2"], distant), CORE)
    r["CY6"] = send(after(r["Y6"], distant), CORE)
    return call_sum(r, close, distant, picks)


def solution(mesh):
    placed = (
        P(),
        P(("groups", "tm"), None),
        P(("groups", "tm"), None, None),
        P(),
        P(("groups", "tm"), None, None),
        P(),
        P(("groups", "tm"), None),
        P(("groups", "tm"), None),
    )
    return jax.shard_map(
        per_device,
        mesh=mesh,
        in_specs=placed,
        out_specs=P(("groups", "tm"), None, None),
        check_vma=False,
    )
```

time: 349 us -> 92.7 us (0.27)
  the two profiles are of different devices: /device:TPU:16 before, /device:TPU:27 now
where the time goes in v2:
time: 92.7 us; the launch traced here: 92.1 us
  Pallas kernels  34.9 us (38%)
  starting transfers between devices  26.1 us (28%)
  waiting for transfers between devices  25.8 us (28%)
  local copies, waits for them, and re-layouts  3.36 us (4%)
  other arithmetic  1.56 us (2%)
    ppermute x24, starting transfers between devices, send(): return lax.ppermute(block, 'tm', route)  26.1 us
    ppermute x24, waiting for transfers between devices, send(): return lax.ppermute(block, 'tm', route)  25.8 us
    pallas_call x6, Pallas kernels, call(): pl.pallas_call(kernel, out_shape=outs, in_specs=[spec] * len(ins), out_sp...  21.2 us
    pallas_call x1, Pallas kernels, call_sum(): pl.pallas_call(functools.partial(sum_kernel, names, cols), out_shape=jax....  13.8 us
    unnamed x8, local copies, waits for them, and re-layouts  3.35 us
  transfers between devices with their start and end apart: 24, of which 7 were waited for; matrix products, arithmetic and copies ran while one was open for 1% of the time, Pallas kernels for 21%

profile of v2, /device:TPU:27, one launch (start us, length us, event | category | flops | bytes accessed | tf_op | source)
XLA Modules:
  0.0 92.1 jit_solution(3881279343142300671)
XLA Ops:
  0.0 0.0 copy-start.3
  0.0 1.6 %shard_map.82 = bf16[1,8,2048]{2,1,0:T(8,128)(2,1)} custom-call(f32[1,1024]{1,0:T(1,128)} %decay.1, s32[1,8,8]{2,1,0:T(8,128)} %mask.1, s32[1,2048]{1,0:T(1,128)} %lanes.1, f32[1,2048]{1,0:T(1,128)} %load.1), custom_call_target="tpu_custom_call" | custom-call | flops 1048576 | bytes 20736 | tf_op jit(solution)/shard_map/pallas_call | solution.py:58
  1.6 0.7 collective-permute-start
  2.3 1.1 %collective-permute-done = bf16[1,8,2048]{2,1,0:T(8,128)(2,1)S(1)} collective-permute-done((bf16[1,8,2048]{2,1,0:T(8,128)(2,1)}, bf16[1,8,2048]{2,1,0:T(8,128)(2,1)S(1)}, u32[]{:S(2)}, u32[]{:S(2)}) %collective-permute-start) | collective-permute-done | bytes 32800 | tf_op jit(solution)/shard_map/ppermute | solution.py:32
  3.4 0.8 fusion
  4.2 1.3 %collective-permute-start.1 = (bf16[2,8,2048]{2,1,0:T(8,128)(2,1)S(1)}, bf16[2,8,2048]{2,1,0:T(8,128)(2,1)S(1)}, u32[]{:S(2)}, u32[]{:S(2)}) collective-permute-start(bf16[2,8,2048]{2,1,0:T(8,128)(2,1)S(1)} %get-tuple-element.76), channel_id=1, source_target_pairs={{1,5},{3,7},{5,9},{7,11},{9,13},{11,15},{17,21},{19,23},{21,25},{2... | collective-permute-start | bytes 196616 | tf_op jit(solution)/shard_map/ppermute | solution.py:32
  5.5 3.7 %collective-permute-done.1 = bf16[2,8,2048]{2,1,0:T(8,128)(2,1)S(1)} collective-permute-done((bf16[2,8,2048]{2,1,0:T(8,128)(2,1)S(1)}, bf16[2,8,2048]{2,1,0:T(8,128)(2,1)S(1)}, u32[]{:S(2)}, u32[]{:S(2)}) %collective-permute-start.1) | collective-permute-done | bytes 65568 | tf_op jit(solution)/shard_map/ppermute | solution.py:32
  9.2 3.1 %collective-permute-start.2 = (bf16[2,2,8,2048]{3,2,1,0:T(8,128)(2,1)S(1)}, bf16[2,2,8,2048]{3,2,1,0:T(8,128)(2,1)S(1)}, u32[]{:S(2)}, u32[]{:S(2)}) collective-permute-start(bf16[2,2,8,2048]{3,2,1,0:T(8,128)(2,1)S(1)} %pad_maximum_fusion.1), channel_id=1, source_target_pairs={{1,3},{3,1},{5,7},{7,5},{9,11},{11,9},{13,15},{15,13},{17,19},{19,... | collective-permute-start | bytes 393224 | tf_op jit(solution)/shard_map/ppermute | solution.py:32
  12.4 0.7 collective-permute-start.5
  13.1 0.7 collective-permute-start.4
  13.8 2.8 %collective-permute-done.2 = bf16[2,2,8,2048]{3,2,1,0:T(8,128)(2,1)S(1)} collective-permute-done((bf16[2,2,8,2048]{3,2,1,0:T(8,128)(2,1)S(1)}, bf16[2,2,8,2048]{3,2,1,0:T(8,128)(2,1)S(1)}, u32[]{:S(2)}, u32[]{:S(2)}) %collective-permute-start.2) | collective-permute-done | bytes 131104 | tf_op jit(solution)/shard_map/ppermute | solution.py:32
  16.7 0.7 pad_maximum_fusion
  17.4 0.0 collective-permute-start.3
  17.4 0.5 collective-permute-start.8
  17.9 0.0 copy-start
  17.9 1.6 %copy-done = bf16[1024,1024]{1,0:T(8,128)(2,1)S(1)} copy-done((bf16[1024,1024]{1,0:T(8,128)(2,1)S(1)}, bf16[1024,1024]{1,0:T(8,128)(2,1)}, u32[]{:S(2)}) %copy-start) | copy-done | bytes 2097176
  19.5 1.0 %copy-done.1 = bf16[1024,256]{1,0:T(8,128)(2,1)S(1)} copy-done((bf16[1024,256]{1,0:T(8,128)(2,1)S(1)}, bf16[1024,256]{1,0:T(8,128)(2,1)}, u32[]{:S(2)}) %copy-start.1) | copy-done | bytes 524312
  20.6 0.0 copy-start.2
  20.6 0.7 copy-done.2
  21.3 0.4 shard_map.83
  21.7 0.0 copy-done.3
  21.7 1.3 %collective-permute-start.9 = (bf16[256,2048]{1,0:T(8,128)(2,1)S(1)}, bf16[256,2048]{1,0:T(8,128)(2,1)S(1)}, u32[]{:S(2)}, u32[]{:S(2)}) collective-permute-start(bf16[256,2048]{1,0:T(8,128)(2,1)S(1)} %bitcast.11), channel_id=1, source_target_pairs={{1,5},{3,7},{5,9},{7,11},{9,13},{11,15},{17,21},{19,23},{21,25},{2... | collective-permute-start | bytes 3145736 | tf_op jit(solution)/shard_map/ppermute | solution.py:32
  23.0 0.0 collective-permute-done.3
  23.1 0.0 collective-permute-done.5.refs_13_
  23.1 0.0 collective-permute-done.4.refs_10_
  23.1 0.7 collective-permute-start.6
  23.8 0.7 collective-permute-start.13
  24.5 4.7 %shard_map.84 = (bf16[1024,1024]{1,0:T(8,128)(2,1)S(1)}, bf16[1024,768]{1,0:T(8,128)(2,1)S(1)}, f32[1024,128]{1,0:T(8,128)S(1)}) custom-call(bf16[2,4,8,2048]{3,2,1,0:T(8,128)(2,1)S(1)} %broadcast_select_fusion.near, bf16[1024,1024]{1,0:T(8,128)(2,1)S(1)} %get-tuple-element.43.c, bf16[1024,384]{1,0:T(8,128)(2,1)S(1)} %get-tuple-element.44.gi, ...), custom_call_target="tpu_custom_call" | custom-call | flops 4294967296 | bytes 3670016 | tf_op jit(solution)/shard_map/pallas_call | solution.py:58
  29.2 9.8 %collective-permute-done.9.refs_11_ = bf16[256,2048]{1,0:T(8,128)(2,1)S(1)} collective-permute-done((bf16[256,2048]{1,0:T(8,128)(2,1)S(1)}, bf16[256,2048]{1,0:T(8,128)(2,1)S(1)}, u32[]{:S(2)}, u32[]{:S(2)}) %collective-permute-start.9) | collective-permute-done | bytes 1048608 | tf_op jit(solution)/shard_map/ppermute | solution.py:32
  39.0 0.0 collective-permute-start.10
  39.0 0.5 collective-permute-start.11
  39.5 0.0 collective-permute-done.8.refs_0_
  39.5 0.7 collective-permute-start.12
  40.2 0.0 collective-permute-done.6.far
  40.2 3.1 %collective-permute-start.20 = (bf16[256,2048]{1,0:T(8,128)(2,1)S(1)}, bf16[256,2048]{1,0:T(8,128)(2,1)S(1)}, u32[]{:S(2)}, u32[]{:S(2)}) collective-permute-start(bf16[256,2048]{1,0:T(8,128)(2,1)S(1)} %collective-permute-done.9.refs_11_), channel_id=1, source_target_pairs={{1,3},{3,1},{5,7},{7,5},{9,11},{11,9},{13,15},{15,13},{17,19},{19,... | collective-permute-start | bytes 3145736 | tf_op jit(solution)/shard_map/ppermute | solution.py:32
  43.4 0.0 collective-permute-done.13.refs_15_
  43.4 0.9 collective-permute-start.7
  44.3 3.7 %shard_map.85 = (bf16[1024,1024]{1,0:T(8,128)(2,1)S(1)}, bf16[1024,1024]{1,0:T(8,128)(2,1)S(1)}, f32[1024,128]{1,0:T(8,128)S(1)}) custom-call(bf16[2,4,8,2048]{3,2,1,0:T(8,128)(2,1)S(1)} %broadcast_select_fusion.near, bf16[1024,1024]{1,0:T(8,128)(2,1)S(1)} %get-tuple-element.43.c, bf16[1024,384]{1,0:T(8,128)(2,1)S(1)} %get-tuple-element.44.gi, ...), custom_call_target="tpu_custom_call" | custom-call | flops 3221225472 | bytes 7340032 | tf_op jit(solution)/shard_map/pallas_call | solution.py:58
  48.0 0.0 collective-permute-done.7.swapped
  48.0 0.1 collective-permute-start.15
  48.1 0.0 collective-permute-done.10.refs_4_
  48.1 0.5 collective-permute-start.14
  48.6 0.0 collective-permute-done.11.refs_1_
  48.6 1.3 %collective-permute-start.22 = (bf16[256,2048]{1,0:T(8,128)(2,1)S(1)}, bf16[256,2048]{1,0:T(8,128)(2,1)S(1)}, u32[]{:S(2)}, u32[]{:S(2)}) collective-permute-start(bf16[256,2048]{1,0:T(8,128)(2,1)S(1)} %collective-permute-done.13.refs_15_), channel_id=1, source_target_pairs={{0,5},{4,9},{8,13},{16,21},{20,25},{24,29}} | collective-permute-start | bytes 3145736 | tf_op jit(solution)/shard_map/ppermute | solution.py:32
  49.8 0.0 collective-permute-done.12.refs_17_
  49.9 1.6 %collective-permute-start.18 = (bf16[256,2048]{1,0:T(8,128)(2,1)S(1)}, bf16[256,2048]{1,0:T(8,128)(2,1)S(1)}, u32[]{:S(2)}, u32[]{:S(2)}) collective-permute-start(bf16[256,2048]{1,0:T(8,128)(2,1)S(1)} %bitcast.12), channel_id=1, source_target_pairs={{1,3},{5,7},{9,11},{13,15},{17,19},{21,23},{25,27},{29,31}} | collective-permute-start | bytes 3145736 | tf_op jit(solution)/shard_map/ppermute | solution.py:32
  51.5 4.5 %collective-permute-done.20.refs_16_ = bf16[256,2048]{1,0:T(8,128)(2,1)S(1)} collective-permute-done((bf16[256,2048]{1,0:T(8,128)(2,1)S(1)}, bf16[256,2048]{1,0:T(8,128)(2,1)S(1)}, u32[]{:S(2)}, u32[]{:S(2)}) %collective-permute-start.20) | collective-permute-done | bytes 1048608 | tf_op jit(solution)/shard_map/ppermute | solution.py:32
  56.1 0.9 collective-permute-start.16
  57.0 5.5 %shard_map.86 = (bf16[1024,768]{1,0:T(8,128)(2,1)S(1)}, bf16[1024,128]{1,0:T(8,128)(2,1)S(1)}, bf16[128,2048]{1,0:T(8,128)(2,1)S(1)}) custom-call(bf16[2,4,8,2048]{3,2,1,0:T(8,128)(2,1)S(1)} %broadcast_select_fusion.near, bf16[4,8,2048]{2,1,0:T(8,128)(2,1)S(1)} %collective-permute-done.6.far, bf16[4,8,2048]{2,1,0:T(8,128)(2,1)S(1)} %collective-permute-done.7.swapped, ...), custom_call_target="tpu_custom_call" | custom-call | flops 4831838208 | bytes 3407872 | tf_op jit(solution)/shard_map/pallas_call | solution.py:58
  62.4 0.0 collective-permute-done.15.refs_2_
  62.4 2.3 %collective-permute-start.21 = (bf16[256,2048]{1,0:T(8,128)(2,1)S(1)}, bf16[256,2048]{1,0:T(8,128)(2,1)S(1)}, u32[]{:S(2)}, u32[]{:S(2)}) collective-permute-start(bf16[256,2048]{1,0:T(8,128)(2,1)S(1)} %collective-permute-done.20.refs_16_), channel_id=1, source_target_pairs={{0,1},{1,0},{2,3},{3,2},{4,5},{5,4},{6,7},{7,6},{8,9},{9,8},{10,11... | collective-permute-start | bytes 3145736 | tf_op jit(solution)/shard_map/ppermute | solution.py:32
  64.8 0.0 collective-permute-done.14.refs_6_
  64.8 5.3 %shard_map.87.refs_20_ = bf16[1024,1152]{1,0:T(8,128)(2,1)S(1)} custom-call(bf16[2,4,8,2048]{3,2,1,0:T(8,128)(2,1)S(1)} %broadcast_select_fusion.near, bf16[1024,1024]{1,0:T(8,128)(2,1)S(1)} %get-tuple-element.43.c, bf16[1024,384]{1,0:T(8,128)(2,1)S(1)} %get-tuple-element.44.gi, bf16[1024,1024]{1,0:T(8,128)(2,1)S(1)} %get-tuple-element.64.p, ...), custom_call_target="tpu_custom_call" | custom-call | flops 536870912 | bytes 7602176 | tf_op jit(solution)/shard_map/pallas_call | solution.py:58
  70.1 0.0 collective-permute-done.22.refs_18_
  70.1 0.1 collective-permute-start.23
  70.2 0.0 collective-permute-done.18.refs_14_
  70.2 0.0 collective-permute-done.16.refs_12_
  70.2 4.2 %collective-permute-start.17 = (bf16[256,2048]{1,0:T(8,128)(2,1)S(1)}, bf16[256,2048]{1,0:T(8,128)(2,1)S(1)}, u32[]{:S(2)}, u32[]{:S(2)}) collective-permute-start(bf16[256,2048]{1,0:T(8,128)(2,1)S(1)} %collective-permute-done.16.refs_12_), channel_id=1, source_target_pairs={{0,1},{1,0},{2,3},{3,2},{4,5},{5,4},{6,7},{7,6},{8,9},{9,8},{10,11... | collective-permute-start | bytes 3145736 | tf_op jit(solution)/shard_map/ppermute | solution.py:32
  74.4 0.0 collective-permute-start.19
  74.4 0.0 collective-permute-done.21.refs_7_
  74.4 0.0 collective-permute-done.23.refs_8_
  74.4 2.3 %collective-permute-done.17.refs_3_ = bf16[256,2048]{1,0:T(8,128)(2,1)S(1)} collective-permute-done((bf16[256,2048]{1,0:T(8,128)(2,1)S(1)}, bf16[256,2048]{1,0:T(8,128)(2,1)S(1)}, u32[]{:S(2)}, u32[]{:S(2)}) %collective-permute-start.17) | collective-permute-done | bytes 1048608 | tf_op jit(solution)/shard_map/ppermute | solution.py:32
  76.7 1.5 %collective-permute-done.19.refs_5_ = bf16[256,2048]{1,0:T(8,128)(2,1)S(1)} collective-permute-done((bf16[256,2048]{1,0:T(8,128)(2,1)S(1)}, bf16[256,2048]{1,0:T(8,128)(2,1)S(1)}, u32[]{:S(2)}, u32[]{:S(2)}) %collective-permute-start.19) | collective-permute-done | bytes 1048608 | tf_op jit(solution)/shard_map/ppermute | solution.py:32
  78.2 13.8 %shard_map.88 = f32[1,1024,2048]{2,1,0:T(8,128)} custom-call(bf16[256,2048]{1,0:T(8,128)(2,1)} %collective-permute-done.8.refs_0_, bf16[256,2048]{1,0:T(8,128)(2,1)S(1)} %collective-permute-done.11.refs_1_, bf16[256,2048]{1,0:T(8,128)(2,1)S(1)} %collective-permute-done.15.refs_2_, bf16[256,2048]{1,0:T(8,128)(2,1)S(1)} %collective-permute-done.17.refs_3_, ...), custom_call_target="tpu_custom_call" | custom-call | flops 9126805504 | bytes 16777216 | tf_op jit(solution)/shard_map/pallas_call | solution.py:272
  (4 shorter events, 0.1 us)
Async XLA Ops:
  0.0 21.7 %copy-start.3 = (bf16[1,256,2048]{2,1,0:T(8,128)(2,1)S(1)}, bf16[1,256,2048]{2,1,0:T(8,128)(2,1)}, u32[]{:S(2)}) copy-start(bf16[1,256,2048]{2,1,0:T(8,128)(2,1)} %param.12) | copy-start | bytes 3145732
  1.6 1.8 %collective-permute-start = (bf16[1,8,2048]{2,1,0:T(8,128)(2,1)}, bf16[1,8,2048]{2,1,0:T(8,128)(2,1)S(1)}, u32[]{:S(2)}, u32[]{:S(2)}) collective-permute-start(bf16[1,8,2048]{2,1,0:T(8,128)(2,1)} %shard_map.82), channel_id=1, source_target_pairs={{0,1},{1,0},{2,3},{3,2},{4,5},{5,4},{6,7},{7,6},{8,9},{9,8},{10,11... | collective-permute-start | bytes 98312 | tf_op jit(solution)/shard_map/ppermute | solution.py:32
  4.2 5.0 %collective-permute-start.1 = (bf16[2,8,2048]{2,1,0:T(8,128)(2,1)S(1)}, bf16[2,8,2048]{2,1,0:T(8,128)(2,1)S(1)}, u32[]{:S(2)}, u32[]{:S(2)}) collective-permute-start(bf16[2,8,2048]{2,1,0:T(8,128)(2,1)S(1)} %get-tuple-element.76), channel_id=1, source_target_pairs={{1,5},{3,7},{5,9},{7,11},{9,13},{11,15},{17,21},{19,23},{21,25},{2... | collective-permute-start | bytes 196616 | tf_op jit(solution)/shard_map/ppermute | solution.py:32
  9.2 7.5 %collective-permute-start.2 = (bf16[2,2,8,2048]{3,2,1,0:T(8,128)(2,1)S(1)}, bf16[2,2,8,2048]{3,2,1,0:T(8,128)(2,1)S(1)}, u32[]{:S(2)}, u32[]{:S(2)}) collective-permute-start(bf16[2,2,8,2048]{3,2,1,0:T(8,128)(2,1)S(1)} %pad_maximum_fusion.1), channel_id=1, source_target_pairs={{1,3},{3,1},{5,7},{7,5},{9,11},{11,9},{13,15},{15,13},{17,19},{19,... | collective-permute-start | bytes 393224 | tf_op jit(solution)/shard_map/ppermute | solution.py:32
  12.4 10.7 %collective-permute-start.5 = (bf16[256,2048]{1,0:T(8,128)(2,1)}, bf16[256,2048]{1,0:T(8,128)(2,1)S(1)}, u32[]{:S(2)}, u32[]{:S(2)}) collective-permute-start(bf16[256,2048]{1,0:T(8,128)(2,1)} %bitcast.8), channel_id=1, source_target_pairs={{0,2},{2,0},{4,6},{6,4},{8,10},{10,8},{12,14},{14,12},{16,18},{18,... | collective-permute-start | bytes 3145736 | tf_op jit(solution)/shard_map/ppermute | solution.py:32
  13.1 10.0 %collective-permute-start.4 = (bf16[256,2048]{1,0:T(8,128)(2,1)}, bf16[256,2048]{1,0:T(8,128)(2,1)S(1)}, u32[]{:S(2)}, u32[]{:S(2)}) collective-permute-start(bf16[256,2048]{1,0:T(8,128)(2,1)} %bitcast.9), channel_id=1, source_target_pairs={{0,4},{2,6},{4,8},{6,10},{8,12},{10,14},{16,20},{18,22},{20,24},{2... | collective-permute-start | bytes 3145736 | tf_op jit(solution)/shard_map/ppermute | solution.py:32
  17.4 5.6 %collective-permute-start.3 = (bf16[2,4,8,2048]{3,2,1,0:T(8,128)(2,1)}, bf16[2,4,8,2048]{3,2,1,0:T(8,128)(2,1)}, u32[]{:S(2)}, u32[]{:S(2)}) collective-permute-start(bf16[2,4,8,2048]{3,2,1,0:T(8,128)(2,1)} %pad_maximum_fusion), channel_id=1, source_target_pairs={{0,1},{1,0},{2,3},{3,2},{4,5},{5,4},{6,7},{7,6},{8,9},{9,8},{10,11... | collective-permute-start | bytes 786440 | tf_op jit(solution)/shard_map/ppermute | solution.py:32
  17.4 22.1 %collective-permute-start.8 = (bf16[256,2048]{1,0:T(8,128)(2,1)}, bf16[256,2048]{1,0:T(8,128)(2,1)}, u32[]{:S(2)}, u32[]{:S(2)}) collective-permute-start(bf16[256,2048]{1,0:T(8,128)(2,1)} %bitcast.10), channel_id=1, source_target_pairs={{0,1},{1,0},{2,3},{3,2},{4,5},{5,4},{6,7},{7,6},{8,9},{9,8},{10,11... | collective-permute-start | bytes 3145736 | tf_op jit(solution)/shard_map/ppermute | solution.py:32
  17.9 1.6 %copy-start = (bf16[1024,1024]{1,0:T(8,128)(2,1)S(1)}, bf16[1024,1024]{1,0:T(8,128)(2,1)}, u32[]{:S(2)}) copy-start(bf16[1024,1024]{1,0:T(8,128)(2,1)} %c.1) | copy-start | bytes 6291460
  19.5 1.0 %copy-start.1 = (bf16[1024,256]{1,0:T(8,128)(2,1)S(1)}, bf16[1024,256]{1,0:T(8,128)(2,1)}, u32[]{:S(2)}) copy-start(bf16[1024,256]{1,0:T(8,128)(2,1)} %gain.1) | copy-start | bytes 1572868
  20.6 0.7 copy-start.2
  21.7 17.2 %collective-permute-start.9 = (bf16[256,2048]{1,0:T(8,128)(2,1)S(1)}, bf16[256,2048]{1,0:T(8,128)(2,1)S(1)}, u32[]{:S(2)}, u32[]{:S(2)}) collective-permute-start(bf16[256,2048]{1,0:T(8,128)(2,1)S(1)} %bitcast.11), channel_id=1, source_target_pairs={{1,5},{3,7},{5,9},{7,11},{9,13},{11,15},{17,21},{19,23},{21,25},{2... | collective-permute-start | bytes 3145736 | tf_op jit(solution)/shard_map/ppermute | solution.py:32
  23.1 17.1 %collective-permute-start.6 = (bf16[4,8,2048]{2,1,0:T(8,128)(2,1)S(1)}, bf16[4,8,2048]{2,1,0:T(8,128)(2,1)S(1)}, u32[]{:S(2)}, u32[]{:S(2)}) collective-permute-start(bf16[4,8,2048]{2,1,0:T(8,128)(2,1)S(1)} %slice_bitcast_fusion), channel_id=1, source_target_pairs={{0,4},{2,6},{4,8},{6,10},{8,12},{10,14},{16,20},{18,22},{20,24},{2... | collective-permute-start | bytes 393224 | tf_op jit(solution)/shard_map/ppermute | solution.py:32
  23.8 19.6 %collective-permute-start.13 = (bf16[256,2048]{1,0:T(8,128)(2,1)S(1)}, bf16[256,2048]{1,0:T(8,128)(2,1)S(1)}, u32[]{:S(2)}, u32[]{:S(2)}) collective-permute-start(bf16[256,2048]{1,0:T(8,128)(2,1)S(1)} %collective-permute-done.4.refs_10_), channel_id=1, source_target_pairs={{0,2},{2,0},{4,6},{6,4},{8,10},{10,8},{12,14},{14,12},{16,18},{18,... | collective-permute-start | bytes 3145736 | tf_op jit(solution)/shard_map/ppermute | solution.py:32
  39.0 9.1 %collective-permute-start.10 = (bf16[256,2048]{1,0:T(8,128)(2,1)S(1)}, bf16[256,2048]{1,0:T(8,128)(2,1)S(1)}, u32[]{:S(2)}, u32[]{:S(2)}) collective-permute-start(bf16[256,2048]{1,0:T(8,128)(2,1)S(1)} %collective-permute-done.5.refs_13_), channel_id=1, source_target_pairs={{0,1},{1,0},{2,3},{3,2},{4,5},{5,4},{6,7},{7,6},{8,9},{9,8},{10,11... | collective-permute-start | bytes 3145736 | tf_op jit(solution)/shard_map/ppermute | solution.py:32
  39.0 9.6 %collective-permute-start.11 = (bf16[256,2048]{1,0:T(8,128)(2,1)S(1)}, bf16[256,2048]{1,0:T(8,128)(2,1)S(1)}, u32[]{:S(2)}, u32[]{:S(2)}) collective-permute-start(bf16[256,2048]{1,0:T(8,128)(2,1)S(1)} %collective-permute-done.4.refs_10_), channel_id=1, source_target_pairs={{0,1},{1,0},{2,3},{3,2},{4,5},{5,4},{6,7},{7,6},{8,9},{9,8},{10,11... | collective-permute-start | bytes 3145736 | tf_op jit(solution)/shard_map/ppermute | solution.py:32
  39.5 10.4 %collective-permute-start.12 = (bf16[256,2048]{1,0:T(8,128)(2,1)S(1)}, bf16[256,2048]{1,0:T(8,128)(2,1)S(1)}, u32[]{:S(2)}, u32[]{:S(2)}) collective-permute-start(bf16[256,2048]{1,0:T(8,128)(2,1)S(1)} %collective-permute-done.9.refs_11_), channel_id=1, source_target_pairs={{1,4},{3,6},{5,8},{7,10},{9,12},{11,14},{17,20},{19,22},{21,24},{2... | collective-permute-start | bytes 3145736 | tf_op jit(solution)/shard_map/ppermute | solution.py:32
  40.2 15.8 %collective-permute-start.20 = (bf16[256,2048]{1,0:T(8,128)(2,1)S(1)}, bf16[256,2048]{1,0:T(8,128)(2,1)S(1)}, u32[]{:S(2)}, u32[]{:S(2)}) collective-permute-start(bf16[256,2048]{1,0:T(8,128)(2,1)S(1)} %collective-permute-done.9.refs_11_), channel_id=1, source_target_pairs={{1,3},{3,1},{5,7},{7,5},{9,11},{11,9},{13,15},{15,13},{17,19},{19,... | collective-permute-start | bytes 3145736 | tf_op jit(solution)/shard_map/ppermute | solution.py:32
  43.4 4.6 %collective-permute-start.7 = (bf16[4,8,2048]{2,1,0:T(8,128)(2,1)S(1)}, bf16[4,8,2048]{2,1,0:T(8,128)(2,1)S(1)}, u32[]{:S(2)}, u32[]{:S(2)}) collective-permute-start(bf16[4,8,2048]{2,1,0:T(8,128)(2,1)S(1)} %collective-permute-done.6.far), channel_id=1, source_target_pairs={{0,1},{1,0},{2,3},{3,2},{4,5},{5,4},{6,7},{7,6},{8,9},{9,8},{10,11... | collective-permute-start | bytes 393224 | tf_op jit(solution)/shard_map/ppermute | solution.py:32
  48.0 14.5 %collective-permute-start.15 = (bf16[256,2048]{1,0:T(8,128)(2,1)S(1)}, bf16[256,2048]{1,0:T(8,128)(2,1)S(1)}, u32[]{:S(2)}, u32[]{:S(2)}) collective-permute-start(bf16[256,2048]{1,0:T(8,128)(2,1)S(1)} %collective-permute-done.9.refs_11_), channel_id=1, source_target_pairs={{0,1},{1,0},{2,3},{3,2},{4,5},{5,4},{6,7},{7,6},{8,9},{9,8},{10,11... | collective-permute-start | bytes 3145736 | tf_op jit(solution)/shard_map/ppermute | solution.py:32
  48.1 16.7 %collective-permute-start.14 = (bf16[256,2048]{1,0:T(8,128)(2,1)S(1)}, bf16[256,2048]{1,0:T(8,128)(2,1)S(1)}, u32[]{:S(2)}, u32[]{:S(2)}) collective-permute-start(bf16[256,2048]{1,0:T(8,128)(2,1)S(1)} %collective-permute-done.13.refs_15_), channel_id=1, source_target_pairs={{0,1},{1,0},{2,3},{3,2},{4,5},{5,4},{6,7},{7,6},{8,9},{9,8},{10,11... | collective-permute-start | bytes 3145736 | tf_op jit(solution)/shard_map/ppermute | solution.py:32
  48.6 21.5 %collective-permute-start.22 = (bf16[256,2048]{1,0:T(8,128)(2,1)S(1)}, bf16[256,2048]{1,0:T(8,128)(2,1)S(1)}, u32[]{:S(2)}, u32[]{:S(2)}) collective-permute-start(bf16[256,2048]{1,0:T(8,128)(2,1)S(1)} %collective-permute-done.13.refs_15_), channel_id=1, source_target_pairs={{0,5},{4,9},{8,13},{16,21},{20,25},{24,29}} | collective-permute-start | bytes 3145736 | tf_op jit(solution)/shard_map/ppermute | solution.py:32
  49.9 20.3 %collective-permute-start.18 = (bf16[256,2048]{1,0:T(8,128)(2,1)S(1)}, bf16[256,2048]{1,0:T(8,128)(2,1)S(1)}, u32[]{:S(2)}, u32[]{:S(2)}) collective-permute-start(bf16[256,2048]{1,0:T(8,128)(2,1)S(1)} %bitcast.12), channel_id=1, source_target_pairs={{1,3},{5,7},{9,11},{13,15},{17,19},{21,23},{25,27},{29,31}} | collective-permute-start | bytes 3145736 | tf_op jit(solution)/shard_map/ppermute | solution.py:32
  56.1 14.1 %collective-permute-start.16 = (bf16[256,2048]{1,0:T(8,128)(2,1)S(1)}, bf16[256,2048]{1,0:T(8,128)(2,1)S(1)}, u32[]{:S(2)}, u32[]{:S(2)}) collective-permute-start(bf16[256,2048]{1,0:T(8,128)(2,1)S(1)} %collective-permute-done.12.refs_17_), channel_id=1, source_target_pairs={{2,0},{6,4},{10,8},{14,12},{18,16},{22,20},{26,24},{30,28}} | collective-permute-start | bytes 3145736 | tf_op jit(solution)/shard_map/ppermute | solution.py:32
  62.4 12.0 %collective-permute-start.21 = (bf16[256,2048]{1,0:T(8,128)(2,1)S(1)}, bf16[256,2048]{1,0:T(8,128)(2,1)S(1)}, u32[]{:S(2)}, u32[]{:S(2)}) collective-permute-start(bf16[256,2048]{1,0:T(8,128)(2,1)S(1)} %collective-permute-done.20.refs_16_), channel_id=1, source_target_pairs={{0,1},{1,0},{2,3},{3,2},{4,5},{5,4},{6,7},{7,6},{8,9},{9,8},{10,11... | collective-permute-start | bytes 3145736 | tf_op jit(solution)/shard_map/ppermute | solution.py:32
  70.1 4.3 %collective-permute-start.23 = (bf16[256,2048]{1,0:T(8,128)(2,1)S(1)}, bf16[256,2048]{1,0:T(8,128)(2,1)S(1)}, u32[]{:S(2)}, u32[]{:S(2)}) collective-permute-start(bf16[256,2048]{1,0:T(8,128)(2,1)S(1)} %collective-permute-done.22.refs_18_), channel_id=1, source_target_pairs={{0,1},{1,0},{2,3},{3,2},{4,5},{5,4},{6,7},{7,6},{8,9},{9,8},{10,11... | collective-permute-start | bytes 3145736 | tf_op jit(solution)/shard_map/ppermute | solution.py:32
  70.2 6.5 %collective-permute-start.17 = (bf16[256,2048]{1,0:T(8,128)(2,1)S(1)}, bf16[256,2048]{1,0:T(8,128)(2,1)S(1)}, u32[]{:S(2)}, u32[]{:S(2)}) collective-permute-start(bf16[256,2048]{1,0:T(8,128)(2,1)S(1)} %collective-permute-done.16.refs_12_), channel_id=1, source_target_pairs={{0,1},{1,0},{2,3},{3,2},{4,5},{5,4},{6,7},{7,6},{8,9},{9,8},{10,11... | collective-permute-start | bytes 3145736 | tf_op jit(solution)/shard_map/ppermute | solution.py:32
  74.4 3.8 %collective-permute-start.19 = (bf16[256,2048]{1,0:T(8,128)(2,1)S(1)}, bf16[256,2048]{1,0:T(8,128)(2,1)S(1)}, u32[]{:S(2)}, u32[]{:S(2)}) collective-permute-start(bf16[256,2048]{1,0:T(8,128)(2,1)S(1)} %collective-permute-done.18.refs_14_), channel_id=1, source_target_pairs={{0,1},{1,0},{2,3},{3,2},{4,5},{5,4},{6,7},{7,6},{8,9},{9,8},{10,11... | collective-permute-start | bytes 3145736 | tf_op jit(solution)/shard_map/ppermute | solution.py:32

commit v3 on v2

--- a/solution.py
+++ b/solution.py
@@ -228,9 +228,24 @@
 }
 
 
-def sum_kernel(names, cols, *refs):
+def near_sum(names, cols, *refs):
     blocks = dict(zip(names, refs[: len(names)]))
-    close, distant, picks, out, outgoing, sems = refs[len(names) :]
+    close, out = refs[len(names) :]
+    j = position()
+    for pos, held in TABLE.items():
+
+        @pl.when(j == pos)
+        def _(held=held):
+            @pl.loop(0, out.shape[1] // cols)
+            def _(i):
+                where = pl.ds(pl.multiple_of(i * cols, cols), cols)
+                readings = [blocks[name][:, where] for name in held[:4]]
+                out[:, where] = times(close[...], jnp.concatenate(readings, axis=0))
+
+
+def far_sum(names, cols, *refs):
+    blocks = dict(zip(names, refs[: len(names)]))
+    distant, picks, start, out, outgoing, sems = refs[len(names) :]
     steps = out.shape[-1] // cols
     j = position()
 
@@ -249,39 +264,52 @@
             @pl.loop(0, steps)
             def _(i):
                 now = lax.rem(i, 2)
-                readings = [blocks[name][:, columns(i)] for name in held]
-                total = times(close[...], jnp.concatenate(readings[:4], axis=0))
-                rest = jnp.concatenate(readings[4:] + [picks[:, columns(i)]], axis=0)
-                total += times(distant[...], rest)
+                readings = [blocks[name][:, columns(i)] for name in held[4:]]
+                rest = jnp.concatenate(readings + [picks[:, columns(i)]], axis=0)
 
                 @pl.when(i >= 2)
                 def _():
                     result(i - 2, now).wait()
 
-                outgoing[now] = total
+                outgoing[now] = start[:, columns(i)] + times(distant[...], rest)
                 result(i, now).start()
 
             for i in range(max(steps - 2, 0), steps):
                 result(i, i % 2).wait()
 
 
-def call_sum(blocks, close, distant, picks):
-    names = sorted({name for held in TABLE.values() for name in held})
-    width, scen = close.shape[0], picks.shape[1]
-    cols = COLS
+def names_of(part):
+    return sorted({name for held in TABLE.values() for name in held[part]})
+
+
+def call_near(blocks, close, scen):
+    names = names_of(slice(0, 4))
     return pl.pallas_call(
-        functools.partial(sum_kernel, names, cols),
+        functools.partial(near_sum, names, COLS),
+        out_shape=jax.ShapeDtypeStruct((close.shape[0], scen), F32),
+        in_specs=[VMEM] * (len(names) + 1),
+        out_specs=VMEM,
+        cost_estimate=pl.CostEstimate(
+            flops=MIB, bytes_accessed=MIB, transcendentals=0
+        ),
+        compiler_params=pltpu.CompilerParams(vmem_limit_bytes=LIMIT),
+    )(*[blocks[n] for n in names], close)
+
+
+def call_far(blocks, distant, picks, start):
+    names = names_of(slice(4, 8))
+    width, scen = start.shape
+    return pl.pallas_call(
+        functools.partial(far_sum, names, COLS),
         out_shape=jax.ShapeDtypeStruct((1, width, scen), F32),
         in_specs=[VMEM] * (len(names) + 3),
         out_specs=ANY,
-        scratch_shapes=[pltpu.VMEM((2, width, cols), F32), pltpu.SemaphoreType.DMA((2,))],
+        scratch_shapes=[pltpu.VMEM((2, width, COLS), F32), pltpu.SemaphoreType.DMA((2,))],
         cost_estimate=pl.CostEstimate(
-            flops=2 * width * scen * (close.shape[1] + distant.shape[1]),
-            bytes_accessed=16 * MIB,
-            transcendentals=0,
+            flops=2 * scen * distant.size, bytes_accessed=16 * MIB, transcendentals=0
         ),
         compiler_params=pltpu.CompilerParams(vmem_limit_bytes=LIMIT),
-    )(*[blocks[n] for n in names], close, distant, picks)
+    )(*[blocks[n] for n in names], distant, picks, start)
 
 
 def per_device(coupling, decay, block_mask, gain, readings, influence, lanes, axle_load):
@@ -307,20 +335,22 @@
     r["CO"] = send(own, CORE)
     pair = jnp.concatenate([record, send(record, CORE)], axis=0)
     pairs = jnp.stack([pair, send(pair, [(1, 1, 1), (3, 3, 1)])])
+    near = jnp.concatenate([pairs, send(pairs, ROW1)], axis=1)
+    near = jnp.where(core == 1, near, send(near, CORE))
+    late = lax.optimization_barrier((near, coupling, gain, influence.T))
+    near = late[0]
     c, gi, spread = call(
         load_kernel, [square, shape((width, sens + 128), BF16), loads],
-        [coupling, gain, influence.T],
+        list(late[1:]),
         [pltpu.VMEM(influence.T.shape, F32), pltpu.SemaphoreType.DMA((3,))],
         flops=MIB, spec=ANY,
     )
-    near = jnp.concatenate([pairs, send(pairs, ROW1)], axis=1)
-    near = jnp.where(core == 1, near, send(near, CORE))
-    near, r["R1"], r["YO1"], c = lax.optimization_barrier((near, r["R1"], r["YO1"], c))
+    near, r["R1"], c = lax.optimization_barrier((near, r["R1"], c))
     r["R2"] = send(after(own, pairs), [(1, 1, 1), (3, 3, 1)])
+    r1 = r["R1"]
     far = send(near[1], [(0, 0, 1), (2, 2, 1)])
-    far = (far, send(far, CORE))
-    r1 = r["R1"]
     r["YR1"] = send(r1, ROW0)
+    near, r["YO1"] = lax.optimization_barrier((near, r["YO1"]))
     p2, close, w = call(
         first_kernel, [square, shape((width, 3 * sens), BF16), loads],
         [near, c, gi, spread], [t_scratch, t_scratch], flops=8 * unit,
@@ -332,33 +362,37 @@
     r["CR2"] = send(r2, CORE)
     r["CR1"] = send(after(r1, p2), CORE)
     r["CYO1"] = send(after(r["YO1"], p2), CORE)
+    r["YO2"] = send(after(own, p2), [(1, 3, 0)])
+    p2, r["YR1"], far = lax.optimization_barrier((p2, r["YR1"], far))
     p3, close, w = call(
         second_kernel, [square, shape((width, 4 * sens), BF16), loads],
         [near, c, gi, p2, close, w], [t_scratch], flops=6 * unit,
     )
     yr1 = r["YR1"] = after(r["YR1"], p3)
+    far = (far, send(after(far, p3), CORE))
     r["Z3"] = send(yr1, [(0, 1, 1)])
     r["CYR1"] = send(yr1, CORE)
-    far, r["CO"], r["CYO1"], r["CR1"], r["Z2"] = lax.optimization_barrier(
-        (far, r["CO"], r["CYO1"], r["CR1"], r["Z2"], p3)
-    )[:5]
+    far, r["CO"], r["CYO1"], r["CR1"], r["YR2"], r["Z2"] = lax.optimization_barrier(
+        (far, r["CO"], r["CYO1"], r["CR1"], r["YR2"], r["Z2"], p3)
+    )[:6]
     r["Y6"] = send(r["Z2"], [(2, 0, 0)])
-    r["YO2"] = send(after(own, r["Z2"]), [(1, 3, 0)])
     f, fw, picks = call(
         far_kernel,
         [shape((width, 3 * sens), BF16), shape((width, 128), BF16), shape((128, scen), BF16)],
-        [near, *far, c, gi], [t_scratch], flops=9 * unit,
-    )
+        [near, *far, c, gi], [t_scratch], flops=4 * unit,
+    )
+    r["CYO2"] = send(after(r["YO2"], f), CORE)
     p3, r["CYR1"], r["CR2"] = lax.optimization_barrier((p3, r["CYR1"], r["CR2"], f))[:3]
     r["CYR2"] = send(r["YR2"], CORE)
     (distant,) = call(
         near_kernel, [shape((width, 4 * sens + 128), BF16)],
-        [near, c, gi, p3, w, f, fw], [t_scratch, t_scratch], flops=unit,
+        [near, c, gi, p3, w, f, fw], [t_scratch, t_scratch], flops=MIB,
     )
     r["CZ3"] = send(after(r["Z3"], distant), CORE)
-    r["CYO2"] = send(after(r["YO2"], distant), CORE)
-    r["CY6"] = send(after(r["Y6"], distant), CORE)
-    return call_sum(r, close, distant, picks)
+    close, r["Y6"] = lax.optimization_barrier((close, r["Y6"], distant))[:2]
+    r["CY6"] = send(r["Y6"], CORE)
+    start = call_near(r, close, scen)
+    return call_far(r, distant, picks, start)
 
 
 def solution(mesh):

time: 92.7 us -> 91.7 us (0.989)
  the two profiles are of different devices: /device:TPU:27 before, /device:TPU:1 now
where the time goes in v3:
time: 91.7 us; the launch traced here: 91.1 us
  Pallas kernels  35.6 us (39%)
  starting transfers between devices  35.2 us (38%)
  waiting for transfers between devices  14.9 us (16%)
  local copies, waits for them, and re-layouts  3.36 us (4%)
  other arithmetic  1.56 us (2%)
    ppermute x24, starting transfers between devices, send(): return lax.ppermute(block, 'tm', route)  35.2 us
    pallas_call x6, Pallas kernels, call(): pl.pallas_call(kernel, out_shape=outs, in_specs=[spec] * len(ins), out_sp...  21.1 us
    ppermute x24, waiting for transfers between devices, send(): return lax.ppermute(block, 'tm', route)  14.9 us
    pallas_call x1, Pallas kernels, call_far(): pl.pallas_call(functools.partial(far_sum, names, COLS), out_shape=jax.Sha...  8.7 us
    pallas_call x1, Pallas kernels, call_near(): pl.pallas_call(functools.partial(near_sum, names, COLS), out_shape=jax.Sh...  5.8 us
    unnamed x8, local copies, waits for them, and re-layouts  3.35 us
  transfers between devices with their start and end apart: 24, of which 7 were waited for; matrix products, arithmetic and copies ran while one was open for 1% of the time, Pallas kernels for 28%

profile of v3, /device:TPU:1, one launch (start us, length us, event | category | flops | bytes accessed | tf_op | source)
XLA Modules:
  0.0 91.1 jit_solution(10798163174428765790)
XLA Ops:
  0.0 1.5 %shard_map.82 = bf16[1,8,2048]{2,1,0:T(8,128)(2,1)} custom-call(f32[1,1024]{1,0:T(1,128)} %decay.1, s32[1,8,8]{2,1,0:T(8,128)} %mask.1, s32[1,2048]{1,0:T(1,128)} %lanes.1, f32[1,2048]{1,0:T(1,128)} %load.1), custom_call_target="tpu_custom_call" | custom-call | flops 1048576 | bytes 20736 | tf_op jit(solution)/shard_map/pallas_call | solution.py:58
  1.5 0.1 collective-permute-start
  1.6 1.4 %collective-permute-done = bf16[1,8,2048]{2,1,0:T(8,128)(2,1)S(1)} collective-permute-done((bf16[1,8,2048]{2,1,0:T(8,128)(2,1)}, bf16[1,8,2048]{2,1,0:T(8,128)(2,1)S(1)}, u32[]{:S(2)}, u32[]{:S(2)}) %collective-permute-start) | collective-permute-done | bytes 32800 | tf_op jit(solution)/shard_map/ppermute | solution.py:32
  3.0 0.8 fusion
  3.8 4.4 %collective-permute-start.1 = (bf16[2,8,2048]{2,1,0:T(8,128)(2,1)S(1)}, bf16[2,8,2048]{2,1,0:T(8,128)(2,1)S(1)}, u32[]{:S(2)}, u32[]{:S(2)}) collective-permute-start(bf16[2,8,2048]{2,1,0:T(8,128)(2,1)S(1)} %get-tuple-element.98), channel_id=1, source_target_pairs={{1,5},{3,7},{5,9},{7,11},{9,13},{11,15},{17,21},{19,23},{21,25},{2... | collective-permute-start | bytes 196616 | tf_op jit(solution)/shard_map/ppermute | solution.py:32
  8.1 1.3 %collective-permute-done.1 = bf16[2,8,2048]{2,1,0:T(8,128)(2,1)S(1)} collective-permute-done((bf16[2,8,2048]{2,1,0:T(8,128)(2,1)S(1)}, bf16[2,8,2048]{2,1,0:T(8,128)(2,1)S(1)}, u32[]{:S(2)}, u32[]{:S(2)}) %collective-permute-start.1) | collective-permute-done | bytes 65568 | tf_op jit(solution)/shard_map/ppermute | solution.py:32
  9.4 0.0 copy-start.1
  9.5 3.3 %collective-permute-start.2 = (bf16[2,2,8,2048]{3,2,1,0:T(8,128)(2,1)S(1)}, bf16[2,2,8,2048]{3,2,1,0:T(8,128)(2,1)S(1)}, u32[]{:S(2)}, u32[]{:S(2)}) collective-permute-start(bf16[2,2,8,2048]{3,2,1,0:T(8,128)(2,1)S(1)} %pad_maximum_fusion.1), channel_id=1, source_target_pairs={{1,3},{3,1},{5,7},{7,5},{9,11},{11,9},{13,15},{15,13},{17,19},{19,... | collective-permute-start | bytes 393224 | tf_op jit(solution)/shard_map/ppermute | solution.py:32
  12.7 0.7 collective-permute-start.4
  13.5 0.7 collective-permute-start.5
  14.2 1.1 %collective-permute-done.2 = bf16[2,2,8,2048]{3,2,1,0:T(8,128)(2,1)S(1)} collective-permute-done((bf16[2,2,8,2048]{3,2,1,0:T(8,128)(2,1)S(1)}, bf16[2,2,8,2048]{3,2,1,0:T(8,128)(2,1)S(1)}, u32[]{:S(2)}, u32[]{:S(2)}) %collective-permute-start.2) | collective-permute-done | bytes 131104 | tf_op jit(solution)/shard_map/ppermute | solution.py:32
  15.3 0.7 pad_maximum_fusion
  16.0 0.0 collective-permute-start.3
  16.0 4.6 %collective-permute-start.6 = (bf16[256,2048]{1,0:T(8,128)(2,1)}, bf16[256,2048]{1,0:T(8,128)(2,1)S(1)}, u32[]{:S(2)}, u32[]{:S(2)}) collective-permute-start(bf16[256,2048]{1,0:T(8,128)(2,1)} %bitcast.9), channel_id=1, source_target_pairs={{1,5},{3,7},{5,9},{7,11},{9,13},{11,15},{17,21},{19,23},{21,25},{2... | collective-permute-start | bytes 3145736 | tf_op jit(solution)/shard_map/ppermute | solution.py:32
  20.6 0.0 collective-permute-done.3
  20.7 0.0 copy-start
  20.7 1.6 %copy-done = bf16[1024,1024]{1,0:T(8,128)(2,1)S(1)} copy-done((bf16[1024,1024]{1,0:T(8,128)(2,1)S(1)}, bf16[1024,1024]{1,0:T(8,128)(2,1)}, u32[]{:S(2)}) %copy-start) | copy-done | bytes 2097176
  22.3 1.0 %copy-done.2 = bf16[1024,256]{1,0:T(8,128)(2,1)S(1)} copy-done((bf16[1024,256]{1,0:T(8,128)(2,1)S(1)}, bf16[1024,256]{1,0:T(8,128)(2,1)}, u32[]{:S(2)}) %copy-start.2) | copy-done | bytes 524312
  23.3 0.7 copy-done.3
  24.0 0.4 shard_map.83
  24.5 0.0 collective-permute-done.4.refs_5_
  24.5 0.7 collective-permute-start.7
  25.2 0.0 copy-done.1
  25.2 2.2 %collective-permute-start.10 = (bf16[256,2048]{1,0:T(8,128)(2,1)S(1)}, bf16[256,2048]{1,0:T(8,128)(2,1)S(1)}, u32[]{:S(2)}, u32[]{:S(2)}) collective-permute-start(bf16[256,2048]{1,0:T(8,128)(2,1)S(1)} %bitcast.10), channel_id=1, source_target_pairs={{0,1},{1,0},{2,3},{3,2},{4,5},{5,4},{6,7},{7,6},{8,9},{9,8},{10,11... | collective-permute-start | bytes 3145736 | tf_op jit(solution)/shard_map/ppermute | solution.py:32
  27.5 0.0 collective-permute-done.5.refs_7_
  27.5 0.7 collective-permute-start.8
  28.2 4.7 %shard_map.84 = (bf16[1024,1024]{1,0:T(8,128)(2,1)S(1)}, bf16[1024,768]{1,0:T(8,128)(2,1)S(1)}, f32[1024,128]{1,0:T(8,128)S(1)}) custom-call(bf16[2,4,8,2048]{3,2,1,0:T(8,128)(2,1)S(1)} %broadcast_select_fusion.near, bf16[1024,1024]{1,0:T(8,128)(2,1)S(1)} %get-tuple-element.58.c, bf16[1024,384]{1,0:T(8,128)(2,1)S(1)} %get-tuple-element.59.gi, ...), custom_call_target="tpu_custom_call" | custom-call | flops 4294967296 | bytes 3670016 | tf_op jit(solution)/shard_map/pallas_call | solution.py:58
  32.8 2.0 %collective-permute-done.6.refs_6_ = bf16[256,2048]{1,0:T(8,128)(2,1)S(1)} collective-permute-done((bf16[256,2048]{1,0:T(8,128)(2,1)}, bf16[256,2048]{1,0:T(8,128)(2,1)S(1)}, u32[]{:S(2)}, u32[]{:S(2)}) %collective-permute-start.6) | collective-permute-done | bytes 1048608 | tf_op jit(solution)/shard_map/ppermute | solution.py:32
  34.8 1.7 %collective-permute-start.11 = (bf16[256,2048]{1,0:T(8,128)(2,1)S(1)}, bf16[256,2048]{1,0:T(8,128)(2,1)S(1)}, u32[]{:S(2)}, u32[]{:S(2)}) collective-permute-start(bf16[256,2048]{1,0:T(8,128)(2,1)S(1)} %collective-permute-done.5.refs_7_), channel_id=1, source_target_pairs={{0,1},{1,0},{2,3},{3,2},{4,5},{5,4},{6,7},{7,6},{8,9},{9,8},{10,11... | collective-permute-start | bytes 3145736 | tf_op jit(solution)/shard_map/ppermute | solution.py:32
  36.5 0.1 collective-permute-start.12
  36.6 0.0 collective-permute-done.8.far
  36.6 3.6 %collective-permute-start.14 = (bf16[256,2048]{1,0:T(8,128)(2,1)S(1)}, bf16[256,2048]{1,0:T(8,128)(2,1)S(1)}, u32[]{:S(2)}, u32[]{:S(2)}) collective-permute-start(bf16[256,2048]{1,0:T(8,128)(2,1)S(1)} %collective-permute-done.6.refs_6_), channel_id=1, source_target_pairs={{1,4},{3,6},{5,8},{7,10},{9,12},{11,14},{17,20},{19,22},{21,24},{2... | collective-permute-start | bytes 3145736 | tf_op jit(solution)/shard_map/ppermute | solution.py:32
  40.2 0.0 collective-permute-done.7.refs_9_.refs_8_
  40.2 2.6 %collective-permute-start.13 = (bf16[256,2048]{1,0:T(8,128)(2,1)S(1)}, bf16[256,2048]{1,0:T(8,128)(2,1)S(1)}, u32[]{:S(2)}, u32[]{:S(2)}) collective-permute-start(bf16[256,2048]{1,0:T(8,128)(2,1)S(1)} %collective-permute-done.6.refs_6_), channel_id=1, source_target_pairs={{1,3},{3,1},{5,7},{7,5},{9,11},{11,9},{13,15},{15,13},{17,19},{19,... | collective-permute-start | bytes 3145736 | tf_op jit(solution)/shard_map/ppermute | solution.py:32
  42.8 3.7 %shard_map.85 = (bf16[1024,1024]{1,0:T(8,128)(2,1)S(1)}, bf16[1024,1024]{1,0:T(8,128)(2,1)S(1)}, f32[1024,128]{1,0:T(8,128)S(1)}) custom-call(bf16[2,4,8,2048]{3,2,1,0:T(8,128)(2,1)S(1)} %broadcast_select_fusion.near, bf16[1024,1024]{1,0:T(8,128)(2,1)S(1)} %get-tuple-element.58.c, bf16[1024,384]{1,0:T(8,128)(2,1)S(1)} %get-tuple-element.59.gi, ...), custom_call_target="tpu_custom_call" | custom-call | flops 3221225472 | bytes 7340032 | tf_op jit(solution)/shard_map/pallas_call | solution.py:58
  46.5 0.0 collective-permute-done.10.refs_0_
  46.5 0.1 collective-permute-start.9
  46.6 0.0 collective-permute-done.11.refs_2_
  46.6 2.8 %collective-permute-start.22 = (bf16[256,2048]{1,0:T(8,128)(2,1)S(1)}, bf16[256,2048]{1,0:T(8,128)(2,1)S(1)}, u32[]{:S(2)}, u32[]{:S(2)}) collective-permute-start(bf16[256,2048]{1,0:T(8,128)(2,1)S(1)} %bitcast.11), channel_id=1, source_target_pairs={{1,3},{5,7},{9,11},{13,15},{17,19},{21,23},{25,27},{29,31}} | collective-permute-start | bytes 3145736 | tf_op jit(solution)/shard_map/ppermute | solution.py:32
  49.4 0.0 collective-permute-done.12.refs_0_
  49.4 0.1 collective-permute-start.17
  49.5 2.4 %collective-permute-done.14.refs_10_ = bf16[256,2048]{1,0:T(8,128)(2,1)S(1)} collective-permute-done((bf16[256,2048]{1,0:T(8,128)(2,1)S(1)}, bf16[256,2048]{1,0:T(8,128)(2,1)S(1)}, u32[]{:S(2)}, u32[]{:S(2)}) %collective-permute-start.14) | collective-permute-done | bytes 1048608 | tf_op jit(solution)/shard_map/ppermute | solution.py:32
  51.9 0.0 collective-permute-start.16
  51.9 3.9 %collective-permute-done.13.refs_10_.refs_9_ = bf16[256,2048]{1,0:T(8,128)(2,1)S(1)} collective-permute-done((bf16[256,2048]{1,0:T(8,128)(2,1)S(1)}, bf16[256,2048]{1,0:T(8,128)(2,1)S(1)}, u32[]{:S(2)}, u32[]{:S(2)}) %collective-permute-start.13) | collective-permute-done | bytes 1048608 | tf_op jit(solution)/shard_map/ppermute | solution.py:32
  55.8 0.7 collective-permute-start.20
  56.5 0.0 collective-permute-done.9.swapped
  56.5 0.9 collective-permute-start.15
  57.4 5.5 %shard_map.86 = (bf16[1024,768]{1,0:T(8,128)(2,1)S(1)}, bf16[1024,128]{1,0:T(8,128)(2,1)S(1)}, bf16[128,2048]{1,0:T(8,128)(2,1)S(1)}) custom-call(bf16[2,4,8,2048]{3,2,1,0:T(8,128)(2,1)S(1)} %broadcast_select_fusion.near, bf16[4,8,2048]{2,1,0:T(8,128)(2,1)S(1)} %collective-permute-done.8.far, bf16[4,8,2048]{2,1,0:T(8,128)(2,1)S(1)} %collective-permute-done.9.swapped, ...), custom_call_target="tpu_custom_call" | custom-call | flops 2147483648 | bytes 3407872 | tf_op jit(solution)/shard_map/pallas_call | solution.py:58
  62.9 2.9 %collective-permute-done.22.refs_8_ = bf16[256,2048]{1,0:T(8,128)(2,1)S(1)} collective-permute-done((bf16[256,2048]{1,0:T(8,128)(2,1)S(1)}, bf16[256,2048]{1,0:T(8,128)(2,1)S(1)}, u32[]{:S(2)}, u32[]{:S(2)}) %collective-permute-start.22) | collective-permute-done | bytes 1048608 | tf_op jit(solution)/shard_map/ppermute | solution.py:32
  65.7 1.0 %collective-permute-start.19 = (bf16[256,2048]{1,0:T(8,128)(2,1)S(1)}, bf16[256,2048]{1,0:T(8,128)(2,1)S(1)}, u32[]{:S(2)}, u32[]{:S(2)}) collective-permute-start(bf16[256,2048]{1,0:T(8,128)(2,1)S(1)} %collective-permute-done.13.refs_10_.refs_9_), channel_id=1, source_target_pairs={{0,1},{1,0},{2,3},{3,2},{4,5},{5,4},{6,7},{7,6},{8,9},{9,8},{10,11... | collective-permute-start | bytes 3145736 | tf_op jit(solution)/shard_map/ppermute | solution.py:32
  66.8 0.0 collective-permute-done.17.refs_1_
  66.8 0.1 collective-permute-start.23
  66.8 0.0 collective-permute-done.16.refs_4_.refs_2_
  66.8 5.3 %shard_map.87.refs_12_ = bf16[1024,1152]{1,0:T(8,128)(2,1)S(1)} custom-call(bf16[2,4,8,2048]{3,2,1,0:T(8,128)(2,1)S(1)} %broadcast_select_fusion.near, bf16[1024,1024]{1,0:T(8,128)(2,1)S(1)} %get-tuple-element.58.c, bf16[1024,384]{1,0:T(8,128)(2,1)S(1)} %get-tuple-element.59.gi, bf16[1024,1024]{1,0:T(8,128)(2,1)S(1)} %get-tuple-element.83.p, ...), custom_call_target="tpu_custom_call" | custom-call | flops 1048576 | bytes 7602176 | tf_op jit(solution)/shard_map/pallas_call | solution.py:58
  72.2 0.0 collective-permute-done.20.refs_11_
  72.2 0.5 collective-permute-start.21
  72.7 0.0 collective-permute-done.15.refs_7_
  72.7 3.7 %collective-permute-start.18 = (bf16[256,2048]{1,0:T(8,128)(2,1)S(1)}, bf16[256,2048]{1,0:T(8,128)(2,1)S(1)}, u32[]{:S(2)}, u32[]{:S(2)}) collective-permute-start(bf16[256,2048]{1,0:T(8,128)(2,1)S(1)} %collective-permute-done.15.refs_7_), channel_id=1, source_target_pairs={{0,1},{1,0},{2,3},{3,2},{4,5},{5,4},{6,7},{7,6},{8,9},{9,8},{10,11... | collective-permute-start | bytes 3145736 | tf_op jit(solution)/shard_map/ppermute | solution.py:32
  76.4 0.0 collective-permute-done.19.refs_5_.refs_3_
  76.4 0.0 collective-permute-done.23.refs_3_
  76.4 5.8 %shard_map.88.refs_14_ = f32[1024,2048]{1,0:T(8,128)S(1)} custom-call(bf16[256,2048]{1,0:T(8,128)(2,1)S(1)} %collective-permute-done.10.refs_0_, bf16[256,2048]{1,0:T(8,128)(2,1)S(1)} %collective-permute-done.17.refs_1_, bf16[256,2048]{1,0:T(8,128)(2,1)S(1)} %collective-permute-done.11.refs_2_, bf16[256,2048]{1,0:T(8,128)(2,1)S(1)} %collective-permute-done.23.refs_3_, ...), custom_call_target="tpu_custom_call" | custom-call | flops 1048576 | bytes 1048576 | tf_op jit(solution)/shard_map/pallas_call | solution.py:287
  82.2 0.0 collective-permute-done.21.refs_4_
  82.3 0.0 collective-permute-done.18.refs_1_
  82.3 8.7 %shard_map.89 = f32[1,1024,2048]{2,1,0:T(8,128)} custom-call(bf16[256,2048]{1,0:T(8,128)(2,1)S(1)} %collective-permute-done.12.refs_0_, bf16[256,2048]{1,0:T(8,128)(2,1)S(1)} %collective-permute-done.18.refs_1_, bf16[256,2048]{1,0:T(8,128)(2,1)S(1)} %collective-permute-done.16.refs_4_.refs_2_, bf16[256,2048]{1,0:T(8,128)(2,1)S(1)} %collective-permute-done.19.refs_5_.refs_3_, ...), custom_call_target="tpu_custom_call" | custom-call | flops 4831838208 | bytes 16777216 | tf_op jit(solution)/shard_map/pallas_call | solution.py:302
  (5 shorter events, 0.1 us)
Async XLA Ops:
  1.5 1.5 %collective-permute-start = (bf16[1,8,2048]{2,1,0:T(8,128)(2,1)}, bf16[1,8,2048]{2,1,0:T(8,128)(2,1)S(1)}, u32[]{:S(2)}, u32[]{:S(2)}) collective-permute-start(bf16[1,8,2048]{2,1,0:T(8,128)(2,1)} %shard_map.82), channel_id=1, source_target_pairs={{0,1},{1,0},{2,3},{3,2},{4,5},{5,4},{6,7},{7,6},{8,9},{9,8},{10,11... | collective-permute-start | bytes 98312 | tf_op jit(solution)/shard_map/ppermute | solution.py:32
  3.8 5.7 %collective-permute-start.1 = (bf16[2,8,2048]{2,1,0:T(8,128)(2,1)S(1)}, bf16[2,8,2048]{2,1,0:T(8,128)(2,1)S(1)}, u32[]{:S(2)}, u32[]{:S(2)}) collective-permute-start(bf16[2,8,2048]{2,1,0:T(8,128)(2,1)S(1)} %get-tuple-element.98), channel_id=1, source_target_pairs={{1,5},{3,7},{5,9},{7,11},{9,13},{11,15},{17,21},{19,23},{21,25},{2... | collective-permute-start | bytes 196616 | tf_op jit(solution)/shard_map/ppermute | solution.py:32
  9.4 15.8 %copy-start.1 = (bf16[1,256,2048]{2,1,0:T(8,128)(2,1)S(1)}, bf16[1,256,2048]{2,1,0:T(8,128)(2,1)}, u32[]{:S(2)}) copy-start(bf16[1,256,2048]{2,1,0:T(8,128)(2,1)} %param.12) | copy-start | bytes 3145732
  9.5 5.8 %collective-permute-start.2 = (bf16[2,2,8,2048]{3,2,1,0:T(8,128)(2,1)S(1)}, bf16[2,2,8,2048]{3,2,1,0:T(8,128)(2,1)S(1)}, u32[]{:S(2)}, u32[]{:S(2)}) collective-permute-start(bf16[2,2,8,2048]{3,2,1,0:T(8,128)(2,1)S(1)} %pad_maximum_fusion.1), channel_id=1, source_target_pairs={{1,3},{3,1},{5,7},{7,5},{9,11},{11,9},{13,15},{15,13},{17,19},{19,... | collective-permute-start | bytes 393224 | tf_op jit(solution)/shard_map/ppermute | solution.py:32
  12.7 11.7 %collective-permute-start.4 = (bf16[256,2048]{1,0:T(8,128)(2,1)}, bf16[256,2048]{1,0:T(8,128)(2,1)S(1)}, u32[]{:S(2)}, u32[]{:S(2)}) collective-permute-start(bf16[256,2048]{1,0:T(8,128)(2,1)} %bitcast.7), channel_id=1, source_target_pairs={{0,4},{2,6},{4,8},{6,10},{8,12},{10,14},{16,20},{18,22},{20,24},{2... | collective-permute-start | bytes 3145736 | tf_op jit(solution)/shard_map/ppermute | solution.py:32
  13.5 14.0 %collective-permute-start.5 = (bf16[256,2048]{1,0:T(8,128)(2,1)}, bf16[256,2048]{1,0:T(8,128)(2,1)S(1)}, u32[]{:S(2)}, u32[]{:S(2)}) collective-permute-start(bf16[256,2048]{1,0:T(8,128)(2,1)} %bitcast.8), channel_id=1, source_target_pairs={{0,2},{2,0},{4,6},{6,4},{8,10},{10,8},{12,14},{14,12},{16,18},{18,... | collective-permute-start | bytes 3145736 | tf_op jit(solution)/shard_map/ppermute | solution.py:32
  16.0 4.6 %collective-permute-start.3 = (bf16[2,4,8,2048]{3,2,1,0:T(8,128)(2,1)}, bf16[2,4,8,2048]{3,2,1,0:T(8,128)(2,1)}, u32[]{:S(2)}, u32[]{:S(2)}) collective-permute-start(bf16[2,4,8,2048]{3,2,1,0:T(8,128)(2,1)} %pad_maximum_fusion), channel_id=1, source_target_pairs={{0,1},{1,0},{2,3},{3,2},{4,5},{5,4},{6,7},{7,6},{8,9},{9,8},{10,11... | collective-permute-start | bytes 786440 | tf_op jit(solution)/shard_map/ppermute | solution.py:32
  16.0 18.8 %collective-permute-start.6 = (bf16[256,2048]{1,0:T(8,128)(2,1)}, bf16[256,2048]{1,0:T(8,128)(2,1)S(1)}, u32[]{:S(2)}, u32[]{:S(2)}) collective-permute-start(bf16[256,2048]{1,0:T(8,128)(2,1)} %bitcast.9), channel_id=1, source_target_pairs={{1,5},{3,7},{5,9},{7,11},{9,13},{11,15},{17,21},{19,23},{21,25},{2... | collective-permute-start | bytes 3145736 | tf_op jit(solution)/shard_map/ppermute | solution.py:32
  20.7 1.6 %copy-start = (bf16[1024,1024]{1,0:T(8,128)(2,1)S(1)}, bf16[1024,1024]{1,0:T(8,128)(2,1)}, u32[]{:S(2)}) copy-start(bf16[1024,1024]{1,0:T(8,128)(2,1)} %c) | copy-start | bytes 6291460
  22.3 1.0 %copy-start.2 = (bf16[1024,256]{1,0:T(8,128)(2,1)S(1)}, bf16[1024,256]{1,0:T(8,128)(2,1)}, u32[]{:S(2)}) copy-start(bf16[1024,256]{1,0:T(8,128)(2,1)} %gain) | copy-start | bytes 1572868
  23.3 0.7 copy-start.3
  24.5 15.7 %collective-permute-start.7 = (bf16[256,2048]{1,0:T(8,128)(2,1)S(1)}, bf16[256,2048]{1,0:T(8,128)(2,1)S(1)}, u32[]{:S(2)}, u32[]{:S(2)}) collective-permute-start(bf16[256,2048]{1,0:T(8,128)(2,1)S(1)} %collective-permute-done.4.refs_5_), channel_id=1, source_target_pairs={{0,2},{2,0},{4,6},{6,4},{8,10},{10,8},{12,14},{14,12},{16,18},{18,... | collective-permute-start | bytes 3145736 | tf_op jit(solution)/shard_map/ppermute | solution.py:32
  25.2 21.3 %collective-permute-start.10 = (bf16[256,2048]{1,0:T(8,128)(2,1)S(1)}, bf16[256,2048]{1,0:T(8,128)(2,1)S(1)}, u32[]{:S(2)}, u32[]{:S(2)}) collective-permute-start(bf16[256,2048]{1,0:T(8,128)(2,1)S(1)} %bitcast.10), channel_id=1, source_target_pairs={{0,1},{1,0},{2,3},{3,2},{4,5},{5,4},{6,7},{7,6},{8,9},{9,8},{10,11... | collective-permute-start | bytes 3145736 | tf_op jit(solution)/shard_map/ppermute | solution.py:32
  27.5 9.1 %collective-permute-start.8 = (bf16[4,8,2048]{2,1,0:T(8,128)(2,1)S(1)}, bf16[4,8,2048]{2,1,0:T(8,128)(2,1)S(1)}, u32[]{:S(2)}, u32[]{:S(2)}) collective-permute-start(bf16[4,8,2048]{2,1,0:T(8,128)(2,1)S(1)} %slice_bitcast_fusion), channel_id=1, source_target_pairs={{0,4},{2,6},{4,8},{6,10},{8,12},{10,14},{16,20},{18,22},{20,24},{2... | collective-permute-start | bytes 393224 | tf_op jit(solution)/shard_map/ppermute | solution.py:32
  34.8 11.8 %collective-permute-start.11 = (bf16[256,2048]{1,0:T(8,128)(2,1)S(1)}, bf16[256,2048]{1,0:T(8,128)(2,1)S(1)}, u32[]{:S(2)}, u32[]{:S(2)}) collective-permute-start(bf16[256,2048]{1,0:T(8,128)(2,1)S(1)} %collective-permute-done.5.refs_7_), channel_id=1, source_target_pairs={{0,1},{1,0},{2,3},{3,2},{4,5},{5,4},{6,7},{7,6},{8,9},{9,8},{10,11... | collective-permute-start | bytes 3145736 | tf_op jit(solution)/shard_map/ppermute | solution.py:32
  36.5 12.8 %collective-permute-start.12 = (bf16[256,2048]{1,0:T(8,128)(2,1)S(1)}, bf16[256,2048]{1,0:T(8,128)(2,1)S(1)}, u32[]{:S(2)}, u32[]{:S(2)}) collective-permute-start(bf16[256,2048]{1,0:T(8,128)(2,1)S(1)} %collective-permute-done.4.refs_5_), channel_id=1, source_target_pairs={{0,1},{1,0},{2,3},{3,2},{4,5},{5,4},{6,7},{7,6},{8,9},{9,8},{10,11... | collective-permute-start | bytes 3145736 | tf_op jit(solution)/shard_map/ppermute | solution.py:32
  36.6 15.2 %collective-permute-start.14 = (bf16[256,2048]{1,0:T(8,128)(2,1)S(1)}, bf16[256,2048]{1,0:T(8,128)(2,1)S(1)}, u32[]{:S(2)}, u32[]{:S(2)}) collective-permute-start(bf16[256,2048]{1,0:T(8,128)(2,1)S(1)} %collective-permute-done.6.refs_6_), channel_id=1, source_target_pairs={{1,4},{3,6},{5,8},{7,10},{9,12},{11,14},{17,20},{19,22},{21,24},{2... | collective-permute-start | bytes 3145736 | tf_op jit(solution)/shard_map/ppermute | solution.py:32
  40.2 15.5 %collective-permute-start.13 = (bf16[256,2048]{1,0:T(8,128)(2,1)S(1)}, bf16[256,2048]{1,0:T(8,128)(2,1)S(1)}, u32[]{:S(2)}, u32[]{:S(2)}) collective-permute-start(bf16[256,2048]{1,0:T(8,128)(2,1)S(1)} %collective-permute-done.6.refs_6_), channel_id=1, source_target_pairs={{1,3},{3,1},{5,7},{7,5},{9,11},{11,9},{13,15},{15,13},{17,19},{19,... | collective-permute-start | bytes 3145736 | tf_op jit(solution)/shard_map/ppermute | solution.py:32
  46.5 10.0 %collective-permute-start.9 = (bf16[4,8,2048]{2,1,0:T(8,128)(2,1)S(1)}, bf16[4,8,2048]{2,1,0:T(8,128)(2,1)S(1)}, u32[]{:S(2)}, u32[]{:S(2)}) collective-permute-start(bf16[4,8,2048]{2,1,0:T(8,128)(2,1)S(1)} %collective-permute-done.8.far), channel_id=1, source_target_pairs={{0,1},{1,0},{2,3},{3,2},{4,5},{5,4},{6,7},{7,6},{8,9},{9,8},{10,11... | collective-permute-start | bytes 393224 | tf_op jit(solution)/shard_map/ppermute | solution.py:32
  46.6 19.1 %collective-permute-start.22 = (bf16[256,2048]{1,0:T(8,128)(2,1)S(1)}, bf16[256,2048]{1,0:T(8,128)(2,1)S(1)}, u32[]{:S(2)}, u32[]{:S(2)}) collective-permute-start(bf16[256,2048]{1,0:T(8,128)(2,1)S(1)} %bitcast.11), channel_id=1, source_target_pairs={{1,3},{5,7},{9,11},{13,15},{17,19},{21,23},{25,27},{29,31}} | collective-permute-start | bytes 3145736 | tf_op jit(solution)/shard_map/ppermute | solution.py:32
  49.4 17.4 %collective-permute-start.17 = (bf16[256,2048]{1,0:T(8,128)(2,1)S(1)}, bf16[256,2048]{1,0:T(8,128)(2,1)S(1)}, u32[]{:S(2)}, u32[]{:S(2)}) collective-permute-start(bf16[256,2048]{1,0:T(8,128)(2,1)S(1)} %collective-permute-done.6.refs_6_), channel_id=1, source_target_pairs={{0,1},{1,0},{2,3},{3,2},{4,5},{5,4},{6,7},{7,6},{8,9},{9,8},{10,11... | collective-permute-start | bytes 3145736 | tf_op jit(solution)/shard_map/ppermute | solution.py:32
  51.9 15.0 %collective-permute-start.16 = (bf16[256,2048]{1,0:T(8,128)(2,1)S(1)}, bf16[256,2048]{1,0:T(8,128)(2,1)S(1)}, u32[]{:S(2)}, u32[]{:S(2)}) collective-permute-start(bf16[256,2048]{1,0:T(8,128)(2,1)S(1)} %collective-permute-done.7.refs_9_.refs_8_), channel_id=1, source_target_pairs={{0,1},{1,0},{2,3},{3,2},{4,5},{5,4},{6,7},{7,6},{8,9},{9,8},{10,11... | collective-permute-start | bytes 3145736 | tf_op jit(solution)/shard_map/ppermute | solution.py:32
  55.8 16.4 %collective-permute-start.20 = (bf16[256,2048]{1,0:T(8,128)(2,1)S(1)}, bf16[256,2048]{1,0:T(8,128)(2,1)S(1)}, u32[]{:S(2)}, u32[]{:S(2)}) collective-permute-start(bf16[256,2048]{1,0:T(8,128)(2,1)S(1)} %collective-permute-done.7.refs_9_.refs_8_), channel_id=1, source_target_pairs={{0,5},{4,9},{8,13},{16,21},{20,25},{24,29}} | collective-permute-start | bytes 3145736 | tf_op jit(solution)/shard_map/ppermute | solution.py:32
  56.5 16.2 %collective-permute-start.15 = (bf16[256,2048]{1,0:T(8,128)(2,1)S(1)}, bf16[256,2048]{1,0:T(8,128)(2,1)S(1)}, u32[]{:S(2)}, u32[]{:S(2)}) collective-permute-start(bf16[256,2048]{1,0:T(8,128)(2,1)S(1)} %collective-permute-done.14.refs_10_), channel_id=1, source_target_pairs={{2,0},{6,4},{10,8},{14,12},{18,16},{22,20},{26,24},{30,28}} | collective-permute-start | bytes 3145736 | tf_op jit(solution)/shard_map/ppermute | solution.py:32
  65.7 10.7 %collective-permute-start.19 = (bf16[256,2048]{1,0:T(8,128)(2,1)S(1)}, bf16[256,2048]{1,0:T(8,128)(2,1)S(1)}, u32[]{:S(2)}, u32[]{:S(2)}) collective-permute-start(bf16[256,2048]{1,0:T(8,128)(2,1)S(1)} %collective-permute-done.13.refs_10_.refs_9_), channel_id=1, source_target_pairs={{0,1},{1,0},{2,3},{3,2},{4,5},{5,4},{6,7},{7,6},{8,9},{9,8},{10,11... | collective-permute-start | bytes 3145736 | tf_op jit(solution)/shard_map/ppermute | solution.py:32
  66.8 9.7 %collective-permute-start.23 = (bf16[256,2048]{1,0:T(8,128)(2,1)S(1)}, bf16[256,2048]{1,0:T(8,128)(2,1)S(1)}, u32[]{:S(2)}, u32[]{:S(2)}) collective-permute-start(bf16[256,2048]{1,0:T(8,128)(2,1)S(1)} %collective-permute-done.22.refs_8_), channel_id=1, source_target_pairs={{0,1},{1,0},{2,3},{3,2},{4,5},{5,4},{6,7},{7,6},{8,9},{9,8},{10,11... | collective-permute-start | bytes 3145736 | tf_op jit(solution)/shard_map/ppermute | solution.py:32
  72.2 10.1 %collective-permute-start.21 = (bf16[256,2048]{1,0:T(8,128)(2,1)S(1)}, bf16[256,2048]{1,0:T(8,128)(2,1)S(1)}, u32[]{:S(2)}, u32[]{:S(2)}) collective-permute-start(bf16[256,2048]{1,0:T(8,128)(2,1)S(1)} %collective-permute-done.20.refs_11_), channel_id=1, source_target_pairs={{0,1},{1,0},{2,3},{3,2},{4,5},{5,4},{6,7},{7,6},{8,9},{9,8},{10,11... | collective-permute-start | bytes 3145736 | tf_op jit(solution)/shard_map/ppermute | solution.py:32
  72.7 9.6 %collective-permute-start.18 = (bf16[256,2048]{1,0:T(8,128)(2,1)S(1)}, bf16[256,2048]{1,0:T(8,128)(2,1)S(1)}, u32[]{:S(2)}, u32[]{:S(2)}) collective-permute-start(bf16[256,2048]{1,0:T(8,128)(2,1)S(1)} %collective-permute-done.15.refs_7_), channel_id=1, source_target_pairs={{0,1},{1,0},{2,3},{3,2},{4,5},{5,4},{6,7},{7,6},{8,9},{9,8},{10,11... | collective-permute-start | bytes 3145736 | tf_op jit(solution)/shard_map/ppermute | solution.py:32

commit v4 on v3

--- a/solution.py
+++ b/solution.py
@@ -14,7 +14,7 @@
 F32 = jnp.float32
 BF16 = jnp.bfloat16
 LAGS = 8
-COLS = 256
+COLS = 512
 ROWS = 8
 
 

time: 91.7 us -> 90.2 us (0.984)
  Pallas kernels: 35.6 us -> 34.1 us
where the time goes in v4:
time: 90.2 us; the launch traced here: 89.7 us
  starting transfers between devices  35.2 us (39%)
  Pallas kernels  34.1 us (38%)
  waiting for transfers between devices  14.9 us (17%)
  local copies, waits for them, and re-layouts  3.36 us (4%)
  other arithmetic  1.56 us (2%)
    ppermute x24, starting transfers between devices, send(): return lax.ppermute(block, 'tm', route)  35.2 us
    pallas_call x6, Pallas kernels, call(): pl.pallas_call(kernel, out_shape=outs, in_specs=[spec] * len(ins), out_sp...  21.1 us
    ppermute x24, waiting for transfers between devices, send(): return lax.ppermute(block, 'tm', route)  14.9 us
    pallas_call x1, Pallas kernels, call_far(): pl.pallas_call(functools.partial(far_sum, names, COLS), out_shape=jax.Sha...  7.8 us
    pallas_call x1, Pallas kernels, call_near(): pl.pallas_call(functools.partial(near_sum, names, COLS), out_shape=jax.Sh...  5.23 us
    unnamed x8, local copies, waits for them, and re-layouts  3.35 us
  transfers between devices with their start and end apart: 24, of which 7 were waited for; matrix products, arithmetic and copies ran while one was open for 1% of the time, Pallas kernels for 28%

profile of v4, /device:TPU:1, one launch (start us, length us, event | category | flops | bytes accessed | tf_op | source)
XLA Modules:
  0.0 89.7 jit_solution(1737591675390663118)
XLA Ops:
  0.0 1.5 %shard_map.82 = bf16[1,8,2048]{2,1,0:T(8,128)(2,1)} custom-call(f32[1,1024]{1,0:T(1,128)} %decay.1, s32[1,8,8]{2,1,0:T(8,128)} %mask.1, s32[1,2048]{1,0:T(1,128)} %lanes.1, f32[1,2048]{1,0:T(1,128)} %load.1), custom_call_target="tpu_custom_call" | custom-call | flops 1048576 | bytes 20736 | tf_op jit(solution)/shard_map/pallas_call | solution.py:58
  1.5 0.1 collective-permute-start
  1.6 1.4 %collective-permute-done = bf16[1,8,2048]{2,1,0:T(8,128)(2,1)S(1)} collective-permute-done((bf16[1,8,2048]{2,1,0:T(8,128)(2,1)}, bf16[1,8,2048]{2,1,0:T(8,128)(2,1)S(1)}, u32[]{:S(2)}, u32[]{:S(2)}) %collective-permute-start) | collective-permute-done | bytes 32800 | tf_op jit(solution)/shard_map/ppermute | solution.py:32
  3.0 0.8 fusion
  3.8 4.4 %collective-permute-start.1 = (bf16[2,8,2048]{2,1,0:T(8,128)(2,1)S(1)}, bf16[2,8,2048]{2,1,0:T(8,128)(2,1)S(1)}, u32[]{:S(2)}, u32[]{:S(2)}) collective-permute-start(bf16[2,8,2048]{2,1,0:T(8,128)(2,1)S(1)} %get-tuple-element.98), channel_id=1, source_target_pairs={{1,5},{3,7},{5,9},{7,11},{9,13},{11,15},{17,21},{19,23},{21,25},{2... | collective-permute-start | bytes 196616 | tf_op jit(solution)/shard_map/ppermute | solution.py:32
  8.1 1.3 %collective-permute-done.1 = bf16[2,8,2048]{2,1,0:T(8,128)(2,1)S(1)} collective-permute-done((bf16[2,8,2048]{2,1,0:T(8,128)(2,1)S(1)}, bf16[2,8,2048]{2,1,0:T(8,128)(2,1)S(1)}, u32[]{:S(2)}, u32[]{:S(2)}) %collective-permute-start.1) | collective-permute-done | bytes 65568 | tf_op jit(solution)/shard_map/ppermute | solution.py:32
  9.4 0.0 copy-start.1
  9.5 3.3 %collective-permute-start.2 = (bf16[2,2,8,2048]{3,2,1,0:T(8,128)(2,1)S(1)}, bf16[2,2,8,2048]{3,2,1,0:T(8,128)(2,1)S(1)}, u32[]{:S(2)}, u32[]{:S(2)}) collective-permute-start(bf16[2,2,8,2048]{3,2,1,0:T(8,128)(2,1)S(1)} %pad_maximum_fusion.1), channel_id=1, source_target_pairs={{1,3},{3,1},{5,7},{7,5},{9,11},{11,9},{13,15},{15,13},{17,19},{19,... | collective-permute-start | bytes 393224 | tf_op jit(solution)/shard_map/ppermute | solution.py:32
  12.7 0.7 collective-permute-start.4
  13.5 0.7 collective-permute-start.5
  14.2 1.1 %collective-permute-done.2 = bf16[2,2,8,2048]{3,2,1,0:T(8,128)(2,1)S(1)} collective-permute-done((bf16[2,2,8,2048]{3,2,1,0:T(8,128)(2,1)S(1)}, bf16[2,2,8,2048]{3,2,1,0:T(8,128)(2,1)S(1)}, u32[]{:S(2)}, u32[]{:S(2)}) %collective-permute-start.2) | collective-permute-done | bytes 131104 | tf_op jit(solution)/shard_map/ppermute | solution.py:32
  15.3 0.7 pad_maximum_fusion
  16.0 0.0 collective-permute-start.3
  16.0 4.6 %collective-permute-start.6 = (bf16[256,2048]{1,0:T(8,128)(2,1)}, bf16[256,2048]{1,0:T(8,128)(2,1)S(1)}, u32[]{:S(2)}, u32[]{:S(2)}) collective-permute-start(bf16[256,2048]{1,0:T(8,128)(2,1)} %bitcast.9), channel_id=1, source_target_pairs={{1,5},{3,7},{5,9},{7,11},{9,13},{11,15},{17,21},{19,23},{21,25},{2... | collective-permute-start | bytes 3145736 | tf_op jit(solution)/shard_map/ppermute | solution.py:32
  20.6 0.0 collective-permute-done.3
  20.7 0.0 copy-start
  20.7 1.6 %copy-done = bf16[1024,1024]{1,0:T(8,128)(2,1)S(1)} copy-done((bf16[1024,1024]{1,0:T(8,128)(2,1)S(1)}, bf16[1024,1024]{1,0:T(8,128)(2,1)}, u32[]{:S(2)}) %copy-start) | copy-done | bytes 2097176
  22.3 1.0 %copy-done.2 = bf16[1024,256]{1,0:T(8,128)(2,1)S(1)} copy-done((bf16[1024,256]{1,0:T(8,128)(2,1)S(1)}, bf16[1024,256]{1,0:T(8,128)(2,1)}, u32[]{:S(2)}) %copy-start.2) | copy-done | bytes 524312
  23.3 0.7 copy-done.3
  24.0 0.4 shard_map.83
  24.5 0.0 collective-permute-done.4.refs_5_
  24.5 0.7 collective-permute-start.7
  25.2 0.0 copy-done.1
  25.2 2.2 %collective-permute-start.10 = (bf16[256,2048]{1,0:T(8,128)(2,1)S(1)}, bf16[256,2048]{1,0:T(8,128)(2,1)S(1)}, u32[]{:S(2)}, u32[]{:S(2)}) collective-permute-start(bf16[256,2048]{1,0:T(8,128)(2,1)S(1)} %bitcast.10), channel_id=1, source_target_pairs={{0,1},{1,0},{2,3},{3,2},{4,5},{5,4},{6,7},{7,6},{8,9},{9,8},{10,11... | collective-permute-start | bytes 3145736 | tf_op jit(solution)/shard_map/ppermute | solution.py:32
  27.5 0.0 collective-permute-done.5.refs_7_
  27.5 0.7 collective-permute-start.8
  28.2 4.7 %shard_map.84 = (bf16[1024,1024]{1,0:T(8,128)(2,1)S(1)}, bf16[1024,768]{1,0:T(8,128)(2,1)S(1)}, f32[1024,128]{1,0:T(8,128)S(1)}) custom-call(bf16[2,4,8,2048]{3,2,1,0:T(8,128)(2,1)S(1)} %broadcast_select_fusion.near, bf16[1024,1024]{1,0:T(8,128)(2,1)S(1)} %get-tuple-element.58.c, bf16[1024,384]{1,0:T(8,128)(2,1)S(1)} %get-tuple-element.59.gi, ...), custom_call_target="tpu_custom_call" | custom-call | flops 4294967296 | bytes 3670016 | tf_op jit(solution)/shard_map/pallas_call | solution.py:58
  32.8 2.0 %collective-permute-done.6.refs_6_ = bf16[256,2048]{1,0:T(8,128)(2,1)S(1)} collective-permute-done((bf16[256,2048]{1,0:T(8,128)(2,1)}, bf16[256,2048]{1,0:T(8,128)(2,1)S(1)}, u32[]{:S(2)}, u32[]{:S(2)}) %collective-permute-start.6) | collective-permute-done | bytes 1048608 | tf_op jit(solution)/shard_map/ppermute | solution.py:32
  34.8 1.7 %collective-permute-start.11 = (bf16[256,2048]{1,0:T(8,128)(2,1)S(1)}, bf16[256,2048]{1,0:T(8,128)(2,1)S(1)}, u32[]{:S(2)}, u32[]{:S(2)}) collective-permute-start(bf16[256,2048]{1,0:T(8,128)(2,1)S(1)} %collective-permute-done.5.refs_7_), channel_id=1, source_target_pairs={{0,1},{1,0},{2,3},{3,2},{4,5},{5,4},{6,7},{7,6},{8,9},{9,8},{10,11... | collective-permute-start | bytes 3145736 | tf_op jit(solution)/shard_map/ppermute | solution.py:32
  36.5 0.1 collective-permute-start.12
  36.6 0.0 collective-permute-done.8.far
  36.6 3.6 %collective-permute-start.14 = (bf16[256,2048]{1,0:T(8,128)(2,1)S(1)}, bf16[256,2048]{1,0:T(8,128)(2,1)S(1)}, u32[]{:S(2)}, u32[]{:S(2)}) collective-permute-start(bf16[256,2048]{1,0:T(8,128)(2,1)S(1)} %collective-permute-done.6.refs_6_), channel_id=1, source_target_pairs={{1,4},{3,6},{5,8},{7,10},{9,12},{11,14},{17,20},{19,22},{21,24},{2... | collective-permute-start | bytes 3145736 | tf_op jit(solution)/shard_map/ppermute | solution.py:32
  40.2 0.0 collective-permute-done.7.refs_9_.refs_8_
  40.2 2.6 %collective-permute-start.13 = (bf16[256,2048]{1,0:T(8,128)(2,1)S(1)}, bf16[256,2048]{1,0:T(8,128)(2,1)S(1)}, u32[]{:S(2)}, u32[]{:S(2)}) collective-permute-start(bf16[256,2048]{1,0:T(8,128)(2,1)S(1)} %collective-permute-done.6.refs_6_), channel_id=1, source_target_pairs={{1,3},{3,1},{5,7},{7,5},{9,11},{11,9},{13,15},{15,13},{17,19},{19,... | collective-permute-start | bytes 3145736 | tf_op jit(solution)/shard_map/ppermute | solution.py:32
  42.8 3.7 %shard_map.85 = (bf16[1024,1024]{1,0:T(8,128)(2,1)S(1)}, bf16[1024,1024]{1,0:T(8,128)(2,1)S(1)}, f32[1024,128]{1,0:T(8,128)S(1)}) custom-call(bf16[2,4,8,2048]{3,2,1,0:T(8,128)(2,1)S(1)} %broadcast_select_fusion.near, bf16[1024,1024]{1,0:T(8,128)(2,1)S(1)} %get-tuple-element.58.c, bf16[1024,384]{1,0:T(8,128)(2,1)S(1)} %get-tuple-element.59.gi, ...), custom_call_target="tpu_custom_call" | custom-call | flops 3221225472 | bytes 7340032 | tf_op jit(solution)/shard_map/pallas_call | solution.py:58
  46.5 0.0 collective-permute-done.10.refs_0_
  46.5 0.1 collective-permute-start.9
  46.6 0.0 collective-permute-done.11.refs_2_
  46.6 2.8 %collective-permute-start.22 = (bf16[256,2048]{1,0:T(8,128)(2,1)S(1)}, bf16[256,2048]{1,0:T(8,128)(2,1)S(1)}, u32[]{:S(2)}, u32[]{:S(2)}) collective-permute-start(bf16[256,2048]{1,0:T(8,128)(2,1)S(1)} %bitcast.11), channel_id=1, source_target_pairs={{1,3},{5,7},{9,11},{13,15},{17,19},{21,23},{25,27},{29,31}} | collective-permute-start | bytes 3145736 | tf_op jit(solution)/shard_map/ppermute | solution.py:32
  49.4 0.0 collective-permute-done.12.refs_0_
  49.4 0.1 collective-permute-start.17
  49.5 2.4 %collective-permute-done.14.refs_10_ = bf16[256,2048]{1,0:T(8,128)(2,1)S(1)} collective-permute-done((bf16[256,2048]{1,0:T(8,128)(2,1)S(1)}, bf16[256,2048]{1,0:T(8,128)(2,1)S(1)}, u32[]{:S(2)}, u32[]{:S(2)}) %collective-permute-start.14) | collective-permute-done | bytes 1048608 | tf_op jit(solution)/shard_map/ppermute | solution.py:32
  51.9 0.0 collective-permute-start.16
  51.9 3.9 %collective-permute-done.13.refs_10_.refs_9_ = bf16[256,2048]{1,0:T(8,128)(2,1)S(1)} collective-permute-done((bf16[256,2048]{1,0:T(8,128)(2,1)S(1)}, bf16[256,2048]{1,0:T(8,128)(2,1)S(1)}, u32[]{:S(2)}, u32[]{:S(2)}) %collective-permute-start.13) | collective-permute-done | bytes 1048608 | tf_op jit(solution)/shard_map/ppermute | solution.py:32
  55.8 0.7 collective-permute-start.20
  56.5 0.0 collective-permute-done.9.swapped
  56.5 0.9 %collective-permute-start.15 = (bf16[256,2048]{1,0:T(8,128)(2,1)S(1)}, bf16[256,2048]{1,0:T(8,128)(2,1)S(1)}, u32[]{:S(2)}, u32[]{:S(2)}) collective-permute-start(bf16[256,2048]{1,0:T(8,128)(2,1)S(1)} %collective-permute-done.14.refs_10_), channel_id=1, source_target_pairs={{2,0},{6,4},{10,8},{14,12},{18,16},{22,20},{26,24},{30,28}} | collective-permute-start | bytes 3145736 | tf_op jit(solution)/shard_map/ppermute | solution.py:32
  57.4 5.5 %shard_map.86 = (bf16[1024,768]{1,0:T(8,128)(2,1)S(1)}, bf16[1024,128]{1,0:T(8,128)(2,1)S(1)}, bf16[128,2048]{1,0:T(8,128)(2,1)S(1)}) custom-call(bf16[2,4,8,2048]{3,2,1,0:T(8,128)(2,1)S(1)} %broadcast_select_fusion.near, bf16[4,8,2048]{2,1,0:T(8,128)(2,1)S(1)} %collective-permute-done.8.far, bf16[4,8,2048]{2,1,0:T(8,128)(2,1)S(1)} %collective-permute-done.9.swapped, ...), custom_call_target="tpu_custom_call" | custom-call | flops 2147483648 | bytes 3407872 | tf_op jit(solution)/shard_map/pallas_call | solution.py:58
  62.9 2.9 %collective-permute-done.22.refs_8_ = bf16[256,2048]{1,0:T(8,128)(2,1)S(1)} collective-permute-done((bf16[256,2048]{1,0:T(8,128)(2,1)S(1)}, bf16[256,2048]{1,0:T(8,128)(2,1)S(1)}, u32[]{:S(2)}, u32[]{:S(2)}) %collective-permute-start.22) | collective-permute-done | bytes 1048608 | tf_op jit(solution)/shard_map/ppermute | solution.py:32
  65.7 1.0 %collective-permute-start.19 = (bf16[256,2048]{1,0:T(8,128)(2,1)S(1)}, bf16[256,2048]{1,0:T(8,128)(2,1)S(1)}, u32[]{:S(2)}, u32[]{:S(2)}) collective-permute-start(bf16[256,2048]{1,0:T(8,128)(2,1)S(1)} %collective-permute-done.13.refs_10_.refs_9_), channel_id=1, source_target_pairs={{0,1},{1,0},{2,3},{3,2},{4,5},{5,4},{6,7},{7,6},{8,9},{9,8},{10,11... | collective-permute-start | bytes 3145736 | tf_op jit(solution)/shard_map/ppermute | solution.py:32
  66.8 0.0 collective-permute-done.17.refs_1_
  66.8 0.1 collective-permute-start.23
  66.8 0.0 collective-permute-done.16.refs_4_.refs_2_
  66.8 5.3 %shard_map.87.refs_12_ = bf16[1024,1152]{1,0:T(8,128)(2,1)S(1)} custom-call(bf16[2,4,8,2048]{3,2,1,0:T(8,128)(2,1)S(1)} %broadcast_select_fusion.near, bf16[1024,1024]{1,0:T(8,128)(2,1)S(1)} %get-tuple-element.58.c, bf16[1024,384]{1,0:T(8,128)(2,1)S(1)} %get-tuple-element.59.gi, bf16[1024,1024]{1,0:T(8,128)(2,1)S(1)} %get-tuple-element.83.p, ...), custom_call_target="tpu_custom_call" | custom-call | flops 1048576 | bytes 7602176 | tf_op jit(solution)/shard_map/pallas_call | solution.py:58
  72.2 0.0 collective-permute-done.20.refs_11_
  72.2 0.5 collective-permute-start.21
  72.7 0.0 collective-permute-done.15.refs_7_
  72.7 3.7 %collective-permute-start.18 = (bf16[256,2048]{1,0:T(8,128)(2,1)S(1)}, bf16[256,2048]{1,0:T(8,128)(2,1)S(1)}, u32[]{:S(2)}, u32[]{:S(2)}) collective-permute-start(bf16[256,2048]{1,0:T(8,128)(2,1)S(1)} %collective-permute-done.15.refs_7_), channel_id=1, source_target_pairs={{0,1},{1,0},{2,3},{3,2},{4,5},{5,4},{6,7},{7,6},{8,9},{9,8},{10,11... | collective-permute-start | bytes 3145736 | tf_op jit(solution)/shard_map/ppermute | solution.py:32
  76.4 0.0 collective-permute-done.19.refs_5_.refs_3_
  76.4 0.0 collective-permute-done.23.refs_3_
  76.4 5.2 %shard_map.88.refs_14_ = f32[1024,2048]{1,0:T(8,128)S(1)} custom-call(bf16[256,2048]{1,0:T(8,128)(2,1)S(1)} %collective-permute-done.10.refs_0_, bf16[256,2048]{1,0:T(8,128)(2,1)S(1)} %collective-permute-done.17.refs_1_, bf16[256,2048]{1,0:T(8,128)(2,1)S(1)} %collective-permute-done.11.refs_2_, bf16[256,2048]{1,0:T(8,128)(2,1)S(1)} %collective-permute-done.23.refs_3_, ...), custom_call_target="tpu_custom_call" | custom-call | flops 1048576 | bytes 1048576 | tf_op jit(solution)/shard_map/pallas_call | solution.py:287
  81.7 0.0 collective-permute-done.21.refs_4_
  81.7 0.0 collective-permute-done.18.refs_1_
  81.7 7.8 %shard_map.89 = f32[1,1024,2048]{2,1,0:T(8,128)} custom-call(bf16[256,2048]{1,0:T(8,128)(2,1)S(1)} %collective-permute-done.12.refs_0_, bf16[256,2048]{1,0:T(8,128)(2,1)S(1)} %collective-permute-done.18.refs_1_, bf16[256,2048]{1,0:T(8,128)(2,1)S(1)} %collective-permute-done.16.refs_4_.refs_2_, bf16[256,2048]{1,0:T(8,128)(2,1)S(1)} %collective-permute-done.19.refs_5_.refs_3_, ...), custom_call_target="tpu_custom_call" | custom-call | flops 4831838208 | bytes 16777216 | tf_op jit(solution)/shard_map/pallas_call | solution.py:302
  (5 shorter events, 0.1 us)
Async XLA Ops:
  1.5 1.5 %collective-permute-start = (bf16[1,8,2048]{2,1,0:T(8,128)(2,1)}, bf16[1,8,2048]{2,1,0:T(8,128)(2,1)S(1)}, u32[]{:S(2)}, u32[]{:S(2)}) collective-permute-start(bf16[1,8,2048]{2,1,0:T(8,128)(2,1)} %shard_map.82), channel_id=1, source_target_pairs={{0,1},{1,0},{2,3},{3,2},{4,5},{5,4},{6,7},{7,6},{8,9},{9,8},{10,11... | collective-permute-start | bytes 98312 | tf_op jit(solution)/shard_map/ppermute | solution.py:32
  3.8 5.7 %collective-permute-start.1 = (bf16[2,8,2048]{2,1,0:T(8,128)(2,1)S(1)}, bf16[2,8,2048]{2,1,0:T(8,128)(2,1)S(1)}, u32[]{:S(2)}, u32[]{:S(2)}) collective-permute-start(bf16[2,8,2048]{2,1,0:T(8,128)(2,1)S(1)} %get-tuple-element.98), channel_id=1, source_target_pairs={{1,5},{3,7},{5,9},{7,11},{9,13},{11,15},{17,21},{19,23},{21,25},{2... | collective-permute-start | bytes 196616 | tf_op jit(solution)/shard_map/ppermute | solution.py:32
  9.4 15.8 %copy-start.1 = (bf16[1,256,2048]{2,1,0:T(8,128)(2,1)S(1)}, bf16[1,256,2048]{2,1,0:T(8,128)(2,1)}, u32[]{:S(2)}) copy-start(bf16[1,256,2048]{2,1,0:T(8,128)(2,1)} %param.12) | copy-start | bytes 3145732
  9.5 5.8 %collective-permute-start.2 = (bf16[2,2,8,2048]{3,2,1,0:T(8,128)(2,1)S(1)}, bf16[2,2,8,2048]{3,2,1,0:T(8,128)(2,1)S(1)}, u32[]{:S(2)}, u32[]{:S(2)}) collective-permute-start(bf16[2,2,8,2048]{3,2,1,0:T(8,128)(2,1)S(1)} %pad_maximum_fusion.1), channel_id=1, source_target_pairs={{1,3},{3,1},{5,7},{7,5},{9,11},{11,9},{13,15},{15,13},{17,19},{19,... | collective-permute-start | bytes 393224 | tf_op jit(solution)/shard_map/ppermute | solution.py:32
  12.7 11.7 %collective-permute-start.4 = (bf16[256,2048]{1,0:T(8,128)(2,1)}, bf16[256,2048]{1,0:T(8,128)(2,1)S(1)}, u32[]{:S(2)}, u32[]{:S(2)}) collective-permute-start(bf16[256,2048]{1,0:T(8,128)(2,1)} %bitcast.7), channel_id=1, source_target_pairs={{0,4},{2,6},{4,8},{6,10},{8,12},{10,14},{16,20},{18,22},{20,24},{2... | collective-permute-start | bytes 3145736 | tf_op jit(solution)/shard_map/ppermute | solution.py:32
  13.5 14.0 %collective-permute-start.5 = (bf16[256,2048]{1,0:T(8,128)(2,1)}, bf16[256,2048]{1,0:T(8,128)(2,1)S(1)}, u32[]{:S(2)}, u32[]{:S(2)}) collective-permute-start(bf16[256,2048]{1,0:T(8,128)(2,1)} %bitcast.8), channel_id=1, source_target_pairs={{0,2},{2,0},{4,6},{6,4},{8,10},{10,8},{12,14},{14,12},{16,18},{18,... | collective-permute-start | bytes 3145736 | tf_op jit(solution)/shard_map/ppermute | solution.py:32
  16.0 4.6 %collective-permute-start.3 = (bf16[2,4,8,2048]{3,2,1,0:T(8,128)(2,1)}, bf16[2,4,8,2048]{3,2,1,0:T(8,128)(2,1)}, u32[]{:S(2)}, u32[]{:S(2)}) collective-permute-start(bf16[2,4,8,2048]{3,2,1,0:T(8,128)(2,1)} %pad_maximum_fusion), channel_id=1, source_target_pairs={{0,1},{1,0},{2,3},{3,2},{4,5},{5,4},{6,7},{7,6},{8,9},{9,8},{10,11... | collective-permute-start | bytes 786440 | tf_op jit(solution)/shard_map/ppermute | solution.py:32
  16.0 18.8 %collective-permute-start.6 = (bf16[256,2048]{1,0:T(8,128)(2,1)}, bf16[256,2048]{1,0:T(8,128)(2,1)S(1)}, u32[]{:S(2)}, u32[]{:S(2)}) collective-permute-start(bf16[256,2048]{1,0:T(8,128)(2,1)} %bitcast.9), channel_id=1, source_target_pairs={{1,5},{3,7},{5,9},{7,11},{9,13},{11,15},{17,21},{19,23},{21,25},{2... | collective-permute-start | bytes 3145736 | tf_op jit(solution)/shard_map/ppermute | solution.py:32
  20.7 1.6 %copy-start = (bf16[1024,1024]{1,0:T(8,128)(2,1)S(1)}, bf16[1024,1024]{1,0:T(8,128)(2,1)}, u32[]{:S(2)}) copy-start(bf16[1024,1024]{1,0:T(8,128)(2,1)} %c) | copy-start | bytes 6291460
  22.3 1.0 %copy-start.2 = (bf16[1024,256]{1,0:T(8,128)(2,1)S(1)}, bf16[1024,256]{1,0:T(8,128)(2,1)}, u32[]{:S(2)}) copy-start(bf16[1024,256]{1,0:T(8,128)(2,1)} %gain) | copy-start | bytes 1572868
  23.3 0.7 copy-start.3
  24.5 15.7 %collective-permute-start.7 = (bf16[256,2048]{1,0:T(8,128)(2,1)S(1)}, bf16[256,2048]{1,0:T(8,128)(2,1)S(1)}, u32[]{:S(2)}, u32[]{:S(2)}) collective-permute-start(bf16[256,2048]{1,0:T(8,128)(2,1)S(1)} %collective-permute-done.4.refs_5_), channel_id=1, source_target_pairs={{0,2},{2,0},{4,6},{6,4},{8,10},{10,8},{12,14},{14,12},{16,18},{18,... | collective-permute-start | bytes 3145736 | tf_op jit(solution)/shard_map/ppermute | solution.py:32
  25.2 21.3 %collective-permute-start.10 = (bf16[256,2048]{1,0:T(8,128)(2,1)S(1)}, bf16[256,2048]{1,0:T(8,128)(2,1)S(1)}, u32[]{:S(2)}, u32[]{:S(2)}) collective-permute-start(bf16[256,2048]{1,0:T(8,128)(2,1)S(1)} %bitcast.10), channel_id=1, source_target_pairs={{0,1},{1,0},{2,3},{3,2},{4,5},{5,4},{6,7},{7,6},{8,9},{9,8},{10,11... | collective-permute-start | bytes 3145736 | tf_op jit(solution)/shard_map/ppermute | solution.py:32
  27.5 9.1 %collective-permute-start.8 = (bf16[4,8,2048]{2,1,0:T(8,128)(2,1)S(1)}, bf16[4,8,2048]{2,1,0:T(8,128)(2,1)S(1)}, u32[]{:S(2)}, u32[]{:S(2)}) collective-permute-start(bf16[4,8,2048]{2,1,0:T(8,128)(2,1)S(1)} %slice_bitcast_fusion), channel_id=1, source_target_pairs={{0,4},{2,6},{4,8},{6,10},{8,12},{10,14},{16,20},{18,22},{20,24},{2... | collective-permute-start | bytes 393224 | tf_op jit(solution)/shard_map/ppermute | solution.py:32
  34.8 11.8 %collective-permute-start.11 = (bf16[256,2048]{1,0:T(8,128)(2,1)S(1)}, bf16[256,2048]{1,0:T(8,128)(2,1)S(1)}, u32[]{:S(2)}, u32[]{:S(2)}) collective-permute-start(bf16[256,2048]{1,0:T(8,128)(2,1)S(1)} %collective-permute-done.5.refs_7_), channel_id=1, source_target_pairs={{0,1},{1,0},{2,3},{3,2},{4,5},{5,4},{6,7},{7,6},{8,9},{9,8},{10,11... | collective-permute-start | bytes 3145736 | tf_op jit(solution)/shard_map/ppermute | solution.py:32
  36.5 12.8 %collective-permute-start.12 = (bf16[256,2048]{1,0:T(8,128)(2,1)S(1)}, bf16[256,2048]{1,0:T(8,128)(2,1)S(1)}, u32[]{:S(2)}, u32[]{:S(2)}) collective-permute-start(bf16[256,2048]{1,0:T(8,128)(2,1)S(1)} %collective-permute-done.4.refs_5_), channel_id=1, source_target_pairs={{0,1},{1,0},{2,3},{3,2},{4,5},{5,4},{6,7},{7,6},{8,9},{9,8},{10,11... | collective-permute-start | bytes 3145736 | tf_op jit(solution)/shard_map/ppermute | solution.py:32
  36.6 15.2 %collective-permute-start.14 = (bf16[256,2048]{1,0:T(8,128)(2,1)S(1)}, bf16[256,2048]{1,0:T(8,128)(2,1)S(1)}, u32[]{:S(2)}, u32[]{:S(2)}) collective-permute-start(bf16[256,2048]{1,0:T(8,128)(2,1)S(1)} %collective-permute-done.6.refs_6_), channel_id=1, source_target_pairs={{1,4},{3,6},{5,8},{7,10},{9,12},{11,14},{17,20},{19,22},{21,24},{2... | collective-permute-start | bytes 3145736 | tf_op jit(solution)/shard_map/ppermute | solution.py:32
  40.2 15.5 %collective-permute-start.13 = (bf16[256,2048]{1,0:T(8,128)(2,1)S(1)}, bf16[256,2048]{1,0:T(8,128)(2,1)S(1)}, u32[]{:S(2)}, u32[]{:S(2)}) collective-permute-start(bf16[256,2048]{1,0:T(8,128)(2,1)S(1)} %collective-permute-done.6.refs_6_), channel_id=1, source_target_pairs={{1,3},{3,1},{5,7},{7,5},{9,11},{11,9},{13,15},{15,13},{17,19},{19,... | collective-permute-start | bytes 3145736 | tf_op jit(solution)/shard_map/ppermute | solution.py:32
  46.5 10.0 %collective-permute-start.9 = (bf16[4,8,2048]{2,1,0:T(8,128)(2,1)S(1)}, bf16[4,8,2048]{2,1,0:T(8,128)(2,1)S(1)}, u32[]{:S(2)}, u32[]{:S(2)}) collective-permute-start(bf16[4,8,2048]{2,1,0:T(8,128)(2,1)S(1)} %collective-permute-done.8.far), channel_id=1, source_target_pairs={{0,1},{1,0},{2,3},{3,2},{4,5},{5,4},{6,7},{7,6},{8,9},{9,8},{10,11... | collective-permute-start | bytes 393224 | tf_op jit(solution)/shard_map/ppermute | solution.py:32
  46.6 19.1 %collective-permute-start.22 = (bf16[256,2048]{1,0:T(8,128)(2,1)S(1)}, bf16[256,2048]{1,0:T(8,128)(2,1)S(1)}, u32[]{:S(2)}, u32[]{:S(2)}) collective-permute-start(bf16[256,2048]{1,0:T(8,128)(2,1)S(1)} %bitcast.11), channel_id=1, source_target_pairs={{1,3},{5,7},{9,11},{13,15},{17,19},{21,23},{25,27},{29,31}} | collective-permute-start | bytes 3145736 | tf_op jit(solution)/shard_map/ppermute | solution.py:32
  49.4 17.4 %collective-permute-start.17 = (bf16[256,2048]{1,0:T(8,128)(2,1)S(1)}, bf16[256,2048]{1,0:T(8,128)(2,1)S(1)}, u32[]{:S(2)}, u32[]{:S(2)}) collective-permute-start(bf16[256,2048]{1,0:T(8,128)(2,1)S(1)} %collective-permute-done.6.refs_6_), channel_id=1, source_target_pairs={{0,1},{1,0},{2,3},{3,2},{4,5},{5,4},{6,7},{7,6},{8,9},{9,8},{10,11... | collective-permute-start | bytes 3145736 | tf_op jit(solution)/shard_map/ppermute | solution.py:32
  51.9 15.0 %collective-permute-start.16 = (bf16[256,2048]{1,0:T(8,128)(2,1)S(1)}, bf16[256,2048]{1,0:T(8,128)(2,1)S(1)}, u32[]{:S(2)}, u32[]{:S(2)}) collective-permute-start(bf16[256,2048]{1,0:T(8,128)(2,1)S(1)} %collective-permute-done.7.refs_9_.refs_8_), channel_id=1, source_target_pairs={{0,1},{1,0},{2,3},{3,2},{4,5},{5,4},{6,7},{7,6},{8,9},{9,8},{10,11... | collective-permute-start | bytes 3145736 | tf_op jit(solution)/shard_map/ppermute | solution.py:32
  55.8 16.4 %collective-permute-start.20 = (bf16[256,2048]{1,0:T(8,128)(2,1)S(1)}, bf16[256,2048]{1,0:T(8,128)(2,1)S(1)}, u32[]{:S(2)}, u32[]{:S(2)}) collective-permute-start(bf16[256,2048]{1,0:T(8,128)(2,1)S(1)} %collective-permute-done.7.refs_9_.refs_8_), channel_id=1, source_target_pairs={{0,5},{4,9},{8,13},{16,21},{20,25},{24,29}} | collective-permute-start | bytes 3145736 | tf_op jit(solution)/shard_map/ppermute | solution.py:32
  56.5 16.2 %collective-permute-start.15 = (bf16[256,2048]{1,0:T(8,128)(2,1)S(1)}, bf16[256,2048]{1,0:T(8,128)(2,1)S(1)}, u32[]{:S(2)}, u32[]{:S(2)}) collective-permute-start(bf16[256,2048]{1,0:T(8,128)(2,1)S(1)} %collective-permute-done.14.refs_10_), channel_id=1, source_target_pairs={{2,0},{6,4},{10,8},{14,12},{18,16},{22,20},{26,24},{30,28}} | collective-permute-start | bytes 3145736 | tf_op jit(solution)/shard_map/ppermute | solution.py:32
  65.7 10.7 %collective-permute-start.19 = (bf16[256,2048]{1,0:T(8,128)(2,1)S(1)}, bf16[256,2048]{1,0:T(8,128)(2,1)S(1)}, u32[]{:S(2)}, u32[]{:S(2)}) collective-permute-start(bf16[256,2048]{1,0:T(8,128)(2,1)S(1)} %collective-permute-done.13.refs_10_.refs_9_), channel_id=1, source_target_pairs={{0,1},{1,0},{2,3},{3,2},{4,5},{5,4},{6,7},{7,6},{8,9},{9,8},{10,11... | collective-permute-start | bytes 3145736 | tf_op jit(solution)/shard_map/ppermute | solution.py:32
  66.8 9.7 %collective-permute-start.23 = (bf16[256,2048]{1,0:T(8,128)(2,1)S(1)}, bf16[256,2048]{1,0:T(8,128)(2,1)S(1)}, u32[]{:S(2)}, u32[]{:S(2)}) collective-permute-start(bf16[256,2048]{1,0:T(8,128)(2,1)S(1)} %collective-permute-done.22.refs_8_), channel_id=1, source_target_pairs={{0,1},{1,0},{2,3},{3,2},{4,5},{5,4},{6,7},{7,6},{8,9},{9,8},{10,11... | collective-permute-start | bytes 3145736 | tf_op jit(solution)/shard_map/ppermute | solution.py:32
  72.2 9.5 %collective-permute-start.21 = (bf16[256,2048]{1,0:T(8,128)(2,1)S(1)}, bf16[256,2048]{1,0:T(8,128)(2,1)S(1)}, u32[]{:S(2)}, u32[]{:S(2)}) collective-permute-start(bf16[256,2048]{1,0:T(8,128)(2,1)S(1)} %collective-permute-done.20.refs_11_), channel_id=1, source_target_pairs={{0,1},{1,0},{2,3},{3,2},{4,5},{5,4},{6,7},{7,6},{8,9},{9,8},{10,11... | collective-permute-start | bytes 3145736 | tf_op jit(solution)/shard_map/ppermute | solution.py:32
  72.7 9.0 %collective-permute-start.18 = (bf16[256,2048]{1,0:T(8,128)(2,1)S(1)}, bf16[256,2048]{1,0:T(8,128)(2,1)S(1)}, u32[]{:S(2)}, u32[]{:S(2)}) collective-permute-start(bf16[256,2048]{1,0:T(8,128)(2,1)S(1)} %collective-permute-done.15.refs_7_), channel_id=1, source_target_pairs={{0,1},{1,0},{2,3},{3,2},{4,5},{5,4},{6,7},{7,6},{8,9},{9,8},{10,11... | collective-permute-start | bytes 3145736 | tf_op jit(solution)/shard_map/ppermute | solution.py:32
